TPU v7x, 128 devices: a whole 4x4x4 slice. The times are simulated.
128 devices in a mesh: gx: 8 (over y, core), gy: 16 (over z, x).
Axes of the slice: x: 4, y: 4, z: 4, core: 2. Of those that a mesh axis runs over, the one named last changes fastest.
Arguments:
- right_side: float32 [256, 512, 256], P('gx', 'gy'), may hold values from -32 to 32
- phase: int32 [256, 512, 256], P('gx', 'gy'), may hold values from 1 to 3
- table: float32 [4], replicated, may hold values from 0.3 to 3
Outputs:
- solution_field: float32 [256, 512, 256], P('gx', 'gy')
- residual: float32 [256, 512, 256], P('gx', 'gy')
- pre_residual: float32 [256, 512, 256], P('gx', 'gy')
- residual_image: float32 [256, 512, 256], P('gx', 'gy')
Inputs may be any that keep to these rules, and one draw needn't show every extreme that they name: `phase`: labels 1 slag, 2 steel, 3 argon plume; label 0 stands for the lining outside the grid.
All inputs are finite; a program needn't handle non-finite values.
Results may differ from a plain program's by a relative error of at most 0.0003.
Values sent between devices are 32-bit elements; how exact they have to be, the bound alone decides.
No kernel may reach another device: no remote copies, remote signals or barrier semaphores. Data moves between devices by JAX's collectives and lax.ppermute only.
A program may use at most 64 MiB of HBM per device.

v0:
```python
import jax
import jax.numpy as jnp
from jax import lax
from jax.sharding import PartitionSpec as P

ITERS = 2


centre_value = 1.1
half_width = 0.9
ratio_sigma = centre_value / half_width
rho_first = 1.0 / ratio_sigma
rho_second = 1.0 / (2.0 * ratio_sigma - rho_first)
rho_third = 1.0 / (2.0 * ratio_sigma - rho_second)
start_scale = 1.0 / centre_value
keep_first = rho_second * rho_first
push_first = 2.0 * rho_second / half_width
keep_second = rho_third * rho_second
push_second = 2.0 * rho_third / half_width


def extended(block, sides, width):
    for axis, dim in sides:
        count = lax.axis_size(axis)
        forward = [(i, i + 1) for i in range(count - 1)]
        backward = [(target, source) for source, target in forward]
        low = lax.ppermute(
            lax.slice_in_dim(block, block.shape[dim] - width, None, axis=dim), axis, forward
        )
        high = lax.ppermute(lax.slice_in_dim(block, 0, width, axis=dim), axis, backward)
        block = jnp.concatenate([low, block, high], axis=dim)
    return block


def harmonic(left, right):
    return 2.0 * left * right / (left + right)


def coupling_set(sigma_padded):
    centre = sigma_padded[1:-1, 1:-1, 1:-1]
    to_west = harmonic(centre, sigma_padded[:-2, 1:-1, 1:-1])
    to_east = harmonic(centre, sigma_padded[2:, 1:-1, 1:-1])
    to_south = harmonic(centre, sigma_padded[1:-1, :-2, 1:-1])
    to_north = harmonic(centre, sigma_padded[1:-1, 2:, 1:-1])
    to_down = harmonic(centre, sigma_padded[1:-1, 1:-1, :-2])
    to_up = harmonic(centre, sigma_padded[1:-1, 1:-1, 2:])
    diagonal = to_west + to_east + to_south + to_north + to_down + to_up
    return (to_west, to_east, to_south, to_north, to_down, to_up, diagonal)


def lookup(labels, table):
    return jnp.where(
        labels == 1,
        table[1],
        jnp.where(labels == 2, table[2], jnp.where(labels == 3, table[3], table[0])),
    )


def operate_ext(padded_xy, couplings):
    to_west, to_east, to_south, to_north, to_down, to_up, diagonal = couplings
    padded_z = jnp.pad(padded_xy, ((0, 0), (0, 0), (1, 1)))
    centre = padded_xy[1:-1, 1:-1]
    beside = (
        to_west * padded_xy[:-2, 1:-1]
        + to_east * padded_xy[2:, 1:-1]
        + to_south * padded_xy[1:-1, :-2]
        + to_north * padded_xy[1:-1, 2:]
        + to_down * padded_z[1:-1, 1:-1, :-2]
        + to_up * padded_z[1:-1, 1:-1, 2:]
    )
    return diagonal * centre - beside


def local(right_side, phase, table):
    labels_ext = extended(phase, (("gx", 0), ("gy", 1)), 1)
    sigma_ext = lookup(jnp.pad(labels_ext, ((0, 0), (0, 0), (1, 1))), table)
    stored_set = coupling_set(sigma_ext)

    def composite(vector):
        set_zero = tuple((member for member in stored_set))
        diagonal = set_zero[6]

        def image_of(field):
            return operate_ext(extended(field, (("gx", 0), ("gy", 1)), 1), set_zero)

        first = start_scale * (vector / diagonal)
        change = keep_first * first + push_first * ((vector - image_of(first)) / diagonal)
        second = first + change
        change = keep_second * change + push_second * ((vector - image_of(second)) / diagonal)
        third = second + change
        return (third, image_of(third))

    solution_field = jnp.zeros_like(right_side)
    residual = right_side
    pre_residual, residual_image = composite(residual)
    image_dir = jnp.zeros_like(right_side)
    pre_dir = jnp.zeros_like(right_side)
    resid_dir = jnp.zeros_like(right_side)
    direction = jnp.zeros_like(right_side)
    energy_prev = jnp.float32(1.0)
    step_prev = jnp.float32(1.0)
    for iteration in range(ITERS):
        energy_now, curvature = lax.psum(
            (jnp.sum(residual * pre_residual), jnp.sum(residual_image * pre_residual)), ("gx", "gy")
        )
        pre_image, double_image = composite(residual_image)
        if iteration == 0:
            step_size = energy_now / curvature
            image_dir = double_image
            pre_dir = pre_image
            resid_dir = residual_image
            direction = pre_residual
        else:
            momentum = energy_now / energy_prev
            step_size = energy_now / (curvature - momentum * energy_now / step_prev)
            image_dir = double_image + momentum * image_dir
            pre_dir = pre_image + momentum * pre_dir
            resid_dir = residual_image + momentum * resid_dir
            direction = pre_residual + momentum * direction
        solution_field = solution_field + step_size * direction
        residual = residual - step_size * resid_dir
        pre_residual = pre_residual - step_size * pre_dir
        residual_image = residual_image - step_size * image_dir
        energy_prev = energy_now
        step_prev = step_size
    return (solution_field, residual, pre_residual, residual_image)


def solution(mesh):
    placed = (P("gx", "gy", None), P("gx", "gy", None), P())
    return jax.shard_map(
        local,
        mesh=mesh,
        in_specs=placed,
        out_specs=(
            P("gx", "gy", None),
            P("gx", "gy", None),
            P("gx", "gy", None),
            P("gx", "gy", None),
        ),
        check_vma=False,
    )
```

profile of v0, /device:TPU:1, one launch (start us, length us, event | category | flops | bytes accessed | tf_op | source)
XLA Modules:
  0.0 359.1 jit_solution(430377248482108931)
XLA Ops:
  1.4 4.6 %collective-permute-start = (s32[1,32,256]{2,1,0:T(8,128)S(1)}, s32[1,32,256]{2,1,0:T(8,128)S(1)}, u32[]{:S(2)}, u32[]{:S(2)}) collective-permute-start(s32[1,32,256]{2,1,0:T(8,128)S(1)} %get-tuple-element.70), channel_id=1, source_target_pairs={{0,16},{16,32},{32,48},{48,64},{64,80},{80,96},{96,112},{1,17},{17... | collective-permute-start | bytes 98312 | tf_op jit(solution)/shard_map/ppermute | solution.py:27
  24.9 3.3 collective-permute-start.4
  30.2 3.3 collective-permute-done.5
  38.0 3.4 collective-permute-done.7
  45.0 3.3 collective-permute-start.8
  50.3 3.3 collective-permute-done.9
  53.7 4.8 %collective-permute-start.10 = (f32[34,1,256]{2,1,0:T(1,128)S(1)}, f32[34,1,256]{2,1,0:T(1,128)S(1)}, u32[]{:S(2)}, u32[]{:S(2)}) collective-permute-start(f32[34,1,256]{2,1,0:T(1,128)S(1)} %get-tuple-element.45), channel_id=1, source_target_pairs={{0,1},{1,2},{2,3},{3,4},{4,5},{5,6},{6,7},{7,8},{8,9},{9,10},{10,1... | collective-permute-start | bytes 104456 | tf_op jit(solution)/shard_map/ppermute | solution.py:27
  59.7 3.7 %collective-permute-done.11 = f32[34,1,256]{2,1,0:T(1,128)S(1)} collective-permute-done((f32[34,1,256]{2,1,0:T(1,128)S(1)}, f32[34,1,256]{2,1,0:T(1,128)S(1)}, u32[]{:S(2)}, u32[]{:S(2)}) %collective-permute-start.11) | collective-permute-done | bytes 34848 | tf_op jit(solution)/shard_map/ppermute | solution.py:30
  75.4 3.7 %collective-permute-start.14 = (f32[34,1,256]{2,1,0:T(1,128)S(1)}, f32[34,1,256]{2,1,0:T(1,128)S(1)}, u32[]{:S(2)}, u32[]{:S(2)}) collective-permute-start(f32[34,1,256]{2,1,0:T(1,128)S(1)} %get-tuple-element.43), channel_id=1, source_target_pairs={{0,1},{1,2},{2,3},{3,4},{4,5},{5,6},{6,7},{7,8},{8,9},{9,10},{10,1... | collective-permute-start | bytes 104456 | tf_op jit(solution)/shard_map/ppermute | solution.py:27
  80.5 3.7 %collective-permute-done.15 = f32[34,1,256]{2,1,0:T(1,128)S(1)} collective-permute-done((f32[34,1,256]{2,1,0:T(1,128)S(1)}, f32[34,1,256]{2,1,0:T(1,128)S(1)}, u32[]{:S(2)}, u32[]{:S(2)}) %collective-permute-start.15) | collective-permute-done | bytes 34848 | tf_op jit(solution)/shard_map/ppermute | solution.py:30
  85.1 3.3 multiply_reduce_fusion.2
  94.2 3.3 collective-permute-done.17
  97.6 3.7 %collective-permute-start.18 = (f32[34,1,256]{2,1,0:T(1,128)S(1)}, f32[34,1,256]{2,1,0:T(1,128)S(1)}, u32[]{:S(2)}, u32[]{:S(2)}) collective-permute-start(f32[34,1,256]{2,1,0:T(1,128)S(1)} %get-tuple-element.41), channel_id=1, source_target_pairs={{0,1},{1,2},{2,3},{3,4},{4,5},{5,6},{6,7},{7,8},{8,9},{9,10},{10,1... | collective-permute-start | bytes 104456 | tf_op jit(solution)/shard_map/ppermute | solution.py:27
  102.8 3.5 collective-permute-done.19
  115.0 3.3 collective-permute-done.21
  118.3 3.7 %collective-permute-start.22 = (f32[34,1,256]{2,1,0:T(1,128)S(1)}, f32[34,1,256]{2,1,0:T(1,128)S(1)}, u32[]{:S(2)}, u32[]{:S(2)}) collective-permute-start(f32[34,1,256]{2,1,0:T(1,128)S(1)} %get-tuple-element.39), channel_id=1, source_target_pairs={{0,1},{1,2},{2,3},{3,4},{4,5},{5,6},{6,7},{7,8},{8,9},{9,10},{10,1... | collective-permute-start | bytes 104456 | tf_op jit(solution)/shard_map/ppermute | solution.py:27
  123.4 3.7 %collective-permute-done.23 = f32[34,1,256]{2,1,0:T(1,128)S(1)} collective-permute-done((f32[34,1,256]{2,1,0:T(1,128)S(1)}, f32[34,1,256]{2,1,0:T(1,128)S(1)}, u32[]{:S(2)}, u32[]{:S(2)}) %collective-permute-start.23) | collective-permute-done | bytes 34848 | tf_op jit(solution)/shard_map/ppermute | solution.py:30
  135.8 3.3 collective-permute-done.25
  139.1 3.7 %collective-permute-start.26 = (f32[34,1,256]{2,1,0:T(1,128)S(1)}, f32[34,1,256]{2,1,0:T(1,128)S(1)}, u32[]{:S(2)}, u32[]{:S(2)}) collective-permute-start(f32[34,1,256]{2,1,0:T(1,128)S(1)} %get-tuple-element.37), channel_id=1, source_target_pairs={{0,1},{1,2},{2,3},{3,4},{4,5},{5,6},{6,7},{7,8},{8,9},{9,10},{10,1... | collective-permute-start | bytes 104456 | tf_op jit(solution)/shard_map/ppermute | solution.py:27
  144.2 68.6 %all-reduce.11 = (f32[]{:T(128)}, f32[]{:T(128)}) all-reduce(f32[]{:T(128)} %get-tuple-element.7, f32[]{:T(128)} %get-tuple-element.6), channel_id=1, replica_groups=mesh['gx'=8,'gy'=16] {'gx','gy'}, use_global_device_ids=true, to_apply=%region_1.2 | all-reduce | flops 2 | bytes 16 | tf_op jit(solution)/shard_map/psum | solution.py:103
  216.5 6.4 %fusion.125 = (f32[32,32,256]{2,1,0:T(8,128)S(1)}, f32[32,32,256]{2,1,0:T(8,128)S(1)}, f32[32,32,256]{2,1,0:T(8,128)}) fusion(f32[32,32,256]{2,1,0:T(8,128)S(1)} %copy-done.7, f32[32,32,256]{2,1,0:T(8,128)S(1)} %copy-done.4, f32[32,32,256]{2,1,0:T(8,128)S(1)} %copy-done.1, f32[32,32,256]{2,1,0:T(8,128)S(1)} %get-tuple-element.27, ...), kind=kLoop, calls=%fused_computation.275 | loop fusion | flops 7864320 | bytes 13766660 | tf_op jit(solution)/shard_map/mul | solution.py:86
  223.0 4.5 %collective-permute-start.28 = (f32[1,32,256]{2,1,0:T(8,128)S(1)}, f32[1,32,256]{2,1,0:T(8,128)S(1)}, u32[]{:S(2)}, u32[]{:S(2)}) collective-permute-start(f32[1,32,256]{2,1,0:T(8,128)S(1)} %get-tuple-element.55), channel_id=1, source_target_pairs={{0,16},{16,32},{32,48},{48,64},{64,80},{80,96},{96,112},{1,17},{17... | collective-permute-start | bytes 98312 | tf_op jit(solution)/shard_map/ppermute | solution.py:27
  229.4 3.3 collective-permute-done.29
  235.3 3.4 collective-permute-done.31
  239.7 3.5 fusion.128
  243.2 3.4 collective-permute-start.32
  248.5 3.3 collective-permute-done.33
  257.7 67.4 %all-reduce.10 = (f32[]{:T(128)}, f32[]{:T(128)}) all-reduce(f32[]{:T(128)} %get-tuple-element.5, f32[]{:T(128)} %get-tuple-element.4), channel_id=1, replica_groups=mesh['gx'=8,'gy'=16] {'gx','gy'}, use_global_device_ids=true, to_apply=%region_5.6 | all-reduce | flops 2 | bytes 16 | tf_op jit(solution)/shard_map/psum | solution.py:103
  331.9 7.3 %multiply_subtract_fusion = (f32[32,32,256]{2,1,0:T(8,128)}, f32[32,32,256]{2,1,0:T(8,128)S(1)}) fusion(f32[32,32,256]{2,1,0:T(8,128)} %copy-done.9, f32[]{:T(128)S(6)} %div.70, f32[]{:T(128)S(6)} %div.72, f32[32,32,256]{2,1,0:T(8,128)} %copy-done.12, f32[]{:T(128)S(6)} %div.66, f32[32,32,256]{2,1,0:T(8,128)} %copy-done.23, f32[32,32,256]{2,1,0:T(8,128)} %copy-done.18, ...), kind=kLoop, calls=%fused_computation.254 | loop fusion | flops 9961472 | bytes 15863820 | tf_op jit(solution)/shard_map/sub | solution.py:122
  339.2 4.2 %collective-permute-start.36 = (f32[1,32,256]{2,1,0:T(8,128)S(1)}, f32[1,32,256]{2,1,0:T(8,128)S(1)}, u32[]{:S(2)}, u32[]{:S(2)}) collective-permute-start(f32[1,32,256]{2,1,0:T(8,128)S(1)} %get-tuple-element.51), channel_id=1, source_target_pairs={{0,16},{16,32},{32,48},{48,64},{64,80},{80,96},{96,112},{1,17},{17... | collective-permute-start | bytes 98312 | tf_op jit(solution)/shard_map/ppermute | solution.py:27
  345.3 3.3 collective-permute-done.37
  355.6 3.5 fusion.5
  (150 shorter events, 101.1 us)
Async XLA Ops:
  1.4 6.5 %collective-permute-start = (s32[1,32,256]{2,1,0:T(8,128)S(1)}, s32[1,32,256]{2,1,0:T(8,128)S(1)}, u32[]{:S(2)}, u32[]{:S(2)}) collective-permute-start(s32[1,32,256]{2,1,0:T(8,128)S(1)} %get-tuple-element.70), channel_id=1, source_target_pairs={{0,16},{16,32},{32,48},{48,64},{64,80},{80,96},{96,112},{1,17},{17... | collective-permute-start | bytes 98312 | tf_op jit(solution)/shard_map/ppermute | solution.py:27
  6.0 5.2 %collective-permute-start.1 = (s32[1,32,256]{2,1,0:T(8,128)S(1)}, s32[1,32,256]{2,1,0:T(8,128)S(1)}, u32[]{:S(2)}, u32[]{:S(2)}) collective-permute-start(s32[1,32,256]{2,1,0:T(8,128)S(1)} %get-tuple-element.69), channel_id=1, source_target_pairs={{16,0},{32,16},{48,32},{64,48},{80,64},{96,80},{112,96},{17,1},{33... | collective-permute-start | bytes 98312 | tf_op jit(solution)/shard_map/ppermute | solution.py:30
  11.3 5.0 %collective-permute-start.2 = (s32[34,1,256]{2,1,0:T(1,128)S(1)}, s32[34,1,256]{2,1,0:T(1,128)S(1)}, u32[]{:S(2)}, u32[]{:S(2)}) collective-permute-start(s32[34,1,256]{2,1,0:T(1,128)S(1)} %get-tuple-element.49), channel_id=1, source_target_pairs={{0,1},{1,2},{2,3},{3,4},{4,5},{5,6},{6,7},{7,8},{8,9},{9,10},{10,1... | collective-permute-start | bytes 104456 | tf_op jit(solution)/shard_map/ppermute | solution.py:27
  24.9 5.3 %collective-permute-start.4 = (f32[1,32,256]{2,1,0:T(8,128)S(1)}, f32[1,32,256]{2,1,0:T(8,128)S(1)}, u32[]{:S(2)}, u32[]{:S(2)}) collective-permute-start(f32[1,32,256]{2,1,0:T(8,128)S(1)} %get-tuple-element.67), channel_id=1, source_target_pairs={{0,16},{16,32},{32,48},{48,64},{64,80},{80,96},{96,112},{1,17},{17... | collective-permute-start | bytes 98312 | tf_op jit(solution)/shard_map/ppermute | solution.py:27
  28.3 5.2 %collective-permute-start.5 = (f32[1,32,256]{2,1,0:T(8,128)S(1)}, f32[1,32,256]{2,1,0:T(8,128)S(1)}, u32[]{:S(2)}, u32[]{:S(2)}) collective-permute-start(f32[1,32,256]{2,1,0:T(8,128)S(1)} %get-tuple-element.68), channel_id=1, source_target_pairs={{16,0},{32,16},{48,32},{64,48},{80,64},{96,80},{112,96},{17,1},{33... | collective-permute-start | bytes 98312 | tf_op jit(solution)/shard_map/ppermute | solution.py:30
  45.0 5.3 %collective-permute-start.8 = (f32[1,32,256]{2,1,0:T(8,128)S(1)}, f32[1,32,256]{2,1,0:T(8,128)S(1)}, u32[]{:S(2)}, u32[]{:S(2)}) collective-permute-start(f32[1,32,256]{2,1,0:T(8,128)S(1)} %get-tuple-element.65), channel_id=1, source_target_pairs={{0,16},{16,32},{32,48},{48,64},{64,80},{80,96},{96,112},{1,17},{17... | collective-permute-start | bytes 98312 | tf_op jit(solution)/shard_map/ppermute | solution.py:27
  48.4 5.2 %collective-permute-start.9 = (f32[1,32,256]{2,1,0:T(8,128)S(1)}, f32[1,32,256]{2,1,0:T(8,128)S(1)}, u32[]{:S(2)}, u32[]{:S(2)}) collective-permute-start(f32[1,32,256]{2,1,0:T(8,128)S(1)} %get-tuple-element.66), channel_id=1, source_target_pairs={{16,0},{32,16},{48,32},{64,48},{80,64},{96,80},{112,96},{17,1},{33... | collective-permute-start | bytes 98312 | tf_op jit(solution)/shard_map/ppermute | solution.py:30
  53.7 6.1 %collective-permute-start.10 = (f32[34,1,256]{2,1,0:T(1,128)S(1)}, f32[34,1,256]{2,1,0:T(1,128)S(1)}, u32[]{:S(2)}, u32[]{:S(2)}) collective-permute-start(f32[34,1,256]{2,1,0:T(1,128)S(1)} %get-tuple-element.45), channel_id=1, source_target_pairs={{0,1},{1,2},{2,3},{3,4},{4,5},{5,6},{6,7},{7,8},{8,9},{9,10},{10,1... | collective-permute-start | bytes 104456 | tf_op jit(solution)/shard_map/ppermute | solution.py:27
  67.1 5.0 %collective-permute-start.12 = (f32[1,32,256]{2,1,0:T(8,128)S(1)}, f32[1,32,256]{2,1,0:T(8,128)S(1)}, u32[]{:S(2)}, u32[]{:S(2)}) collective-permute-start(f32[1,32,256]{2,1,0:T(8,128)S(1)} %get-tuple-element.63), channel_id=1, source_target_pairs={{0,16},{16,32},{32,48},{48,64},{64,80},{80,96},{96,112},{1,17},{17... | collective-permute-start | bytes 98312 | tf_op jit(solution)/shard_map/ppermute | solution.py:27
  70.1 5.2 %collective-permute-start.13 = (f32[1,32,256]{2,1,0:T(8,128)S(1)}, f32[1,32,256]{2,1,0:T(8,128)S(1)}, u32[]{:S(2)}, u32[]{:S(2)}) collective-permute-start(f32[1,32,256]{2,1,0:T(8,128)S(1)} %get-tuple-element.64), channel_id=1, source_target_pairs={{16,0},{32,16},{48,32},{64,48},{80,64},{96,80},{112,96},{17,1},{33... | collective-permute-start | bytes 98312 | tf_op jit(solution)/shard_map/ppermute | solution.py:30
  75.4 5.1 %collective-permute-start.14 = (f32[34,1,256]{2,1,0:T(1,128)S(1)}, f32[34,1,256]{2,1,0:T(1,128)S(1)}, u32[]{:S(2)}, u32[]{:S(2)}) collective-permute-start(f32[34,1,256]{2,1,0:T(1,128)S(1)} %get-tuple-element.43), channel_id=1, source_target_pairs={{0,1},{1,2},{2,3},{3,4},{4,5},{5,6},{6,7},{7,8},{8,9},{9,10},{10,1... | collective-permute-start | bytes 104456 | tf_op jit(solution)/shard_map/ppermute | solution.py:27
  79.2 5.0 %collective-permute-start.15 = (f32[34,1,256]{2,1,0:T(1,128)S(1)}, f32[34,1,256]{2,1,0:T(1,128)S(1)}, u32[]{:S(2)}, u32[]{:S(2)}) collective-permute-start(f32[34,1,256]{2,1,0:T(1,128)S(1)} %get-tuple-element.44), channel_id=1, source_target_pairs={{1,0},{2,1},{3,2},{4,3},{5,4},{6,5},{7,6},{8,7},{9,8},{10,9},{11,1... | collective-permute-start | bytes 104456 | tf_op jit(solution)/shard_map/ppermute | solution.py:30
  89.2 5.0 %collective-permute-start.16 = (f32[1,32,256]{2,1,0:T(8,128)S(1)}, f32[1,32,256]{2,1,0:T(8,128)S(1)}, u32[]{:S(2)}, u32[]{:S(2)}) collective-permute-start(f32[1,32,256]{2,1,0:T(8,128)S(1)} %get-tuple-element.61), channel_id=1, source_target_pairs={{0,16},{16,32},{32,48},{48,64},{64,80},{80,96},{96,112},{1,17},{17... | collective-permute-start | bytes 98312 | tf_op jit(solution)/shard_map/ppermute | solution.py:27
  92.3 5.2 %collective-permute-start.17 = (f32[1,32,256]{2,1,0:T(8,128)S(1)}, f32[1,32,256]{2,1,0:T(8,128)S(1)}, u32[]{:S(2)}, u32[]{:S(2)}) collective-permute-start(f32[1,32,256]{2,1,0:T(8,128)S(1)} %get-tuple-element.62), channel_id=1, source_target_pairs={{16,0},{32,16},{48,32},{64,48},{80,64},{96,80},{112,96},{17,1},{33... | collective-permute-start | bytes 98312 | tf_op jit(solution)/shard_map/ppermute | solution.py:30
  97.6 5.2 %collective-permute-start.18 = (f32[34,1,256]{2,1,0:T(1,128)S(1)}, f32[34,1,256]{2,1,0:T(1,128)S(1)}, u32[]{:S(2)}, u32[]{:S(2)}) collective-permute-start(f32[34,1,256]{2,1,0:T(1,128)S(1)} %get-tuple-element.41), channel_id=1, source_target_pairs={{0,1},{1,2},{2,3},{3,4},{4,5},{5,6},{6,7},{7,8},{8,9},{9,10},{10,1... | collective-permute-start | bytes 104456 | tf_op jit(solution)/shard_map/ppermute | solution.py:27
  101.3 5.0 %collective-permute-start.19 = (f32[34,1,256]{2,1,0:T(1,128)S(1)}, f32[34,1,256]{2,1,0:T(1,128)S(1)}, u32[]{:S(2)}, u32[]{:S(2)}) collective-permute-start(f32[34,1,256]{2,1,0:T(1,128)S(1)} %get-tuple-element.42), channel_id=1, source_target_pairs={{1,0},{2,1},{3,2},{4,3},{5,4},{6,5},{7,6},{8,7},{9,8},{10,9},{11,1... | collective-permute-start | bytes 104456 | tf_op jit(solution)/shard_map/ppermute | solution.py:30
  110.0 5.0 %collective-permute-start.20 = (f32[1,32,256]{2,1,0:T(8,128)S(1)}, f32[1,32,256]{2,1,0:T(8,128)S(1)}, u32[]{:S(2)}, u32[]{:S(2)}) collective-permute-start(f32[1,32,256]{2,1,0:T(8,128)S(1)} %get-tuple-element.59), channel_id=1, source_target_pairs={{0,16},{16,32},{32,48},{48,64},{64,80},{80,96},{96,112},{1,17},{17... | collective-permute-start | bytes 98312 | tf_op jit(solution)/shard_map/ppermute | solution.py:27
  113.0 5.2 %collective-permute-start.21 = (f32[1,32,256]{2,1,0:T(8,128)S(1)}, f32[1,32,256]{2,1,0:T(8,128)S(1)}, u32[]{:S(2)}, u32[]{:S(2)}) collective-permute-start(f32[1,32,256]{2,1,0:T(8,128)S(1)} %get-tuple-element.60), channel_id=1, source_target_pairs={{16,0},{32,16},{48,32},{64,48},{80,64},{96,80},{112,96},{17,1},{33... | collective-permute-start | bytes 98312 | tf_op jit(solution)/shard_map/ppermute | solution.py:30
  118.3 5.1 %collective-permute-start.22 = (f32[34,1,256]{2,1,0:T(1,128)S(1)}, f32[34,1,256]{2,1,0:T(1,128)S(1)}, u32[]{:S(2)}, u32[]{:S(2)}) collective-permute-start(f32[34,1,256]{2,1,0:T(1,128)S(1)} %get-tuple-element.39), channel_id=1, source_target_pairs={{0,1},{1,2},{2,3},{3,4},{4,5},{5,6},{6,7},{7,8},{8,9},{9,10},{10,1... | collective-permute-start | bytes 104456 | tf_op jit(solution)/shard_map/ppermute | solution.py:27
  122.1 5.0 %collective-permute-start.23 = (f32[34,1,256]{2,1,0:T(1,128)S(1)}, f32[34,1,256]{2,1,0:T(1,128)S(1)}, u32[]{:S(2)}, u32[]{:S(2)}) collective-permute-start(f32[34,1,256]{2,1,0:T(1,128)S(1)} %get-tuple-element.40), channel_id=1, source_target_pairs={{1,0},{2,1},{3,2},{4,3},{5,4},{6,5},{7,6},{8,7},{9,8},{10,9},{11,1... | collective-permute-start | bytes 104456 | tf_op jit(solution)/shard_map/ppermute | solution.py:30
  130.8 5.0 %collective-permute-start.24 = (f32[1,32,256]{2,1,0:T(8,128)S(1)}, f32[1,32,256]{2,1,0:T(8,128)S(1)}, u32[]{:S(2)}, u32[]{:S(2)}) collective-permute-start(f32[1,32,256]{2,1,0:T(8,128)S(1)} %get-tuple-element.57), channel_id=1, source_target_pairs={{0,16},{16,32},{32,48},{48,64},{64,80},{80,96},{96,112},{1,17},{17... | collective-permute-start | bytes 98312 | tf_op jit(solution)/shard_map/ppermute | solution.py:27
  133.8 5.2 %collective-permute-start.25 = (f32[1,32,256]{2,1,0:T(8,128)S(1)}, f32[1,32,256]{2,1,0:T(8,128)S(1)}, u32[]{:S(2)}, u32[]{:S(2)}) collective-permute-start(f32[1,32,256]{2,1,0:T(8,128)S(1)} %get-tuple-element.58), channel_id=1, source_target_pairs={{16,0},{32,16},{48,32},{64,48},{80,64},{96,80},{112,96},{17,1},{33... | collective-permute-start | bytes 98312 | tf_op jit(solution)/shard_map/ppermute | solution.py:30
  139.1 75.0 %collective-permute-start.26 = (f32[34,1,256]{2,1,0:T(1,128)S(1)}, f32[34,1,256]{2,1,0:T(1,128)S(1)}, u32[]{:S(2)}, u32[]{:S(2)}) collective-permute-start(f32[34,1,256]{2,1,0:T(1,128)S(1)} %get-tuple-element.37), channel_id=1, source_target_pairs={{0,1},{1,2},{2,3},{3,4},{4,5},{5,6},{6,7},{7,8},{8,9},{9,10},{10,1... | collective-permute-start | bytes 104456 | tf_op jit(solution)/shard_map/ppermute | solution.py:27
  142.9 71.3 %collective-permute-start.27 = (f32[34,1,256]{2,1,0:T(1,128)S(1)}, f32[34,1,256]{2,1,0:T(1,128)S(1)}, u32[]{:S(2)}, u32[]{:S(2)}) collective-permute-start(f32[34,1,256]{2,1,0:T(1,128)S(1)} %get-tuple-element.38), channel_id=1, source_target_pairs={{1,0},{2,1},{3,2},{4,3},{5,4},{6,5},{7,6},{8,7},{9,8},{10,9},{11,1... | collective-permute-start | bytes 104456 | tf_op jit(solution)/shard_map/ppermute | solution.py:30
  223.0 6.4 %collective-permute-start.28 = (f32[1,32,256]{2,1,0:T(8,128)S(1)}, f32[1,32,256]{2,1,0:T(8,128)S(1)}, u32[]{:S(2)}, u32[]{:S(2)}) collective-permute-start(f32[1,32,256]{2,1,0:T(8,128)S(1)} %get-tuple-element.55), channel_id=1, source_target_pairs={{0,16},{16,32},{32,48},{48,64},{64,80},{80,96},{96,112},{1,17},{17... | collective-permute-start | bytes 98312 | tf_op jit(solution)/shard_map/ppermute | solution.py:27
  227.4 5.2 %collective-permute-start.29 = (f32[1,32,256]{2,1,0:T(8,128)S(1)}, f32[1,32,256]{2,1,0:T(8,128)S(1)}, u32[]{:S(2)}, u32[]{:S(2)}) collective-permute-start(f32[1,32,256]{2,1,0:T(8,128)S(1)} %get-tuple-element.56), channel_id=1, source_target_pairs={{16,0},{32,16},{48,32},{64,48},{80,64},{96,80},{112,96},{17,1},{33... | collective-permute-start | bytes 98312 | tf_op jit(solution)/shard_map/ppermute | solution.py:30
  243.2 5.3 %collective-permute-start.32 = (f32[1,32,256]{2,1,0:T(8,128)S(1)}, f32[1,32,256]{2,1,0:T(8,128)S(1)}, u32[]{:S(2)}, u32[]{:S(2)}) collective-permute-start(f32[1,32,256]{2,1,0:T(8,128)S(1)} %get-tuple-element.53), channel_id=1, source_target_pairs={{0,16},{16,32},{32,48},{48,64},{64,80},{80,96},{96,112},{1,17},{17... | collective-permute-start | bytes 98312 | tf_op jit(solution)/shard_map/ppermute | solution.py:27
  246.6 5.2 %collective-permute-start.33 = (f32[1,32,256]{2,1,0:T(8,128)S(1)}, f32[1,32,256]{2,1,0:T(8,128)S(1)}, u32[]{:S(2)}, u32[]{:S(2)}) collective-permute-start(f32[1,32,256]{2,1,0:T(8,128)S(1)} %get-tuple-element.54), channel_id=1, source_target_pairs={{16,0},{32,16},{48,32},{64,48},{80,64},{96,80},{112,96},{17,1},{33... | collective-permute-start | bytes 98312 | tf_op jit(solution)/shard_map/ppermute | solution.py:30
  251.9 77.7 %collective-permute-start.34 = (f32[34,1,256]{2,1,0:T(1,128)S(1)}, f32[34,1,256]{2,1,0:T(1,128)S(1)}, u32[]{:S(2)}, u32[]{:S(2)}) collective-permute-start(f32[34,1,256]{2,1,0:T(1,128)S(1)} %get-tuple-element.33), channel_id=1, source_target_pairs={{0,1},{1,2},{2,3},{3,4},{4,5},{5,6},{6,7},{7,8},{8,9},{9,10},{10,1... | collective-permute-start | bytes 104456 | tf_op jit(solution)/shard_map/ppermute | solution.py:27
  254.9 74.6 %collective-permute-start.35 = (f32[34,1,256]{2,1,0:T(1,128)S(1)}, f32[34,1,256]{2,1,0:T(1,128)S(1)}, u32[]{:S(2)}, u32[]{:S(2)}) collective-permute-start(f32[34,1,256]{2,1,0:T(1,128)S(1)} %get-tuple-element.34), channel_id=1, source_target_pairs={{1,0},{2,1},{3,2},{4,3},{5,4},{6,5},{7,6},{8,7},{9,8},{10,9},{11,1... | collective-permute-start | bytes 104456 | tf_op jit(solution)/shard_map/ppermute | solution.py:30
  339.2 6.1 %collective-permute-start.36 = (f32[1,32,256]{2,1,0:T(8,128)S(1)}, f32[1,32,256]{2,1,0:T(8,128)S(1)}, u32[]{:S(2)}, u32[]{:S(2)}) collective-permute-start(f32[1,32,256]{2,1,0:T(8,128)S(1)} %get-tuple-element.51), channel_id=1, source_target_pairs={{0,16},{16,32},{32,48},{48,64},{64,80},{80,96},{96,112},{1,17},{17... | collective-permute-start | bytes 98312 | tf_op jit(solution)/shard_map/ppermute | solution.py:27
  343.4 5.2 %collective-permute-start.37 = (f32[1,32,256]{2,1,0:T(8,128)S(1)}, f32[1,32,256]{2,1,0:T(8,128)S(1)}, u32[]{:S(2)}, u32[]{:S(2)}) collective-permute-start(f32[1,32,256]{2,1,0:T(8,128)S(1)} %get-tuple-element.52), channel_id=1, source_target_pairs={{16,0},{32,16},{48,32},{64,48},{80,64},{96,80},{112,96},{17,1},{33... | collective-permute-start | bytes 98312 | tf_op jit(solution)/shard_map/ppermute | solution.py:30
  (34 other events, 657.5 us)
where the time goes:
time: 361 us; the launch traced here: 359 us
  blocking collectives  136 us (38%)
  starting transfers between devices  99.6 us (28%)
  waiting for transfers between devices  57 us (16%)
  other arithmetic  56.1 us (16%)
  between operations  7.42 us (2%)
    psum x2, blocking collectives, local(): lax.psum((jnp.sum(residual * pre_residual), jnp.sum(residual_image * pre_...  136 us
    ppermute x20, starting transfers between devices, extended(): lax.ppermute(lax.slice_in_dim(block, block.shape[dim] - width, None, axis...  67.1 us
    ppermute x20, waiting for transfers between devices, extended(): lax.ppermute(lax.slice_in_dim(block, 0, width, axis=dim), axis, backward)  57 us
    ppermute x20, starting transfers between devices, extended(): lax.ppermute(lax.slice_in_dim(block, 0, width, axis=dim), axis, backward)  32.5 us
    concatenate x10, other arithmetic, extended(): block = jnp.concatenate([low, block, high], axis=dim)  11.3 us
    mul x3, other arithmetic, composite(): first = start_scale * (vector / diagonal)  9.5 us
    add x3, other arithmetic, composite(): second = first + change  8.92 us
    sub x1, other arithmetic, local(): pre_residual = pre_residual - step_size * pre_dir  7.26 us
  transfers between devices with their start and end apart: 40, of which 18 were waited for; matrix products, arithmetic and copies ran while one was open for 1% of the time, Pallas kernels for 0%

commit v1 on v0

v1 whole, which is shorter than its diff:
```python
import jax
import jax.numpy as jnp
from jax import lax
from jax.experimental import pallas as pl
from jax.experimental.pallas import tpu as pltpu
from jax.sharding import PartitionSpec as P

centre_value = 1.1
half_width = 0.9
ratio_sigma = centre_value / half_width
rho_first = 1.0 / ratio_sigma
rho_second = 1.0 / (2.0 * ratio_sigma - rho_first)
rho_third = 1.0 / (2.0 * ratio_sigma - rho_second)
start_scale = 1.0 / centre_value
keep_first = rho_second * rho_first
push_first = 2.0 * rho_second / half_width
keep_second = rho_third * rho_second
push_second = 2.0 * rho_third / half_width

ZT = (1.0 + keep_first - push_first) * start_scale + push_first
ZS = push_first * start_scale
UZ = 1.0 + keep_second - push_second
UT = push_second - keep_second * start_scale
US = push_second

NB = 32
HB = 9
HL = 10
OFF = 12
YE = 56
XE = NB + 2 * HL
NZ = 256
VM = pl.BlockSpec(memory_space=pltpu.VMEM)
SM = pl.BlockSpec(memory_space=pltpu.SMEM)
f32 = jnp.float32


def shape(*dims):
    return jax.ShapeDtypeStruct(dims, f32)


def params(**more):
    return pltpu.CompilerParams(vmem_limit_bytes=60 * 1024 * 1024, **more)


def pack_kernel(rhs, phase, up, down):
    for x in range(NB):
        up[HB * x:HB * x + HB, :] = rhs[x, NB - HB:NB, :]
        down[HB * x:HB * x + HB, :] = rhs[x, 0:HB, :]
        lo = NB * HB + HL * x
        up[lo:lo + HL, :] = phase[x, NB - HL:NB, :].astype(f32)
        down[lo:lo + HL, :] = phase[x, 0:HL, :].astype(f32)


def join_kernel(rhs, phase, low, high, field, label, up, down):
    zero = jnp.zeros((OFF, NZ), f32)
    for x in range(NB):
        field[x, 0:OFF, :] = zero
        field[x, YE - OFF:YE, :] = zero
        label[x, 0:OFF, :] = zero
        label[x, YE - OFF:YE, :] = zero
        field[x, OFF:OFF + NB, :] = rhs[x]
        label[x, OFF:OFF + NB, :] = phase[x].astype(f32)
        field[x, OFF - HB:OFF, :] = low[HB * x:HB * x + HB, :]
        field[x, OFF + NB:OFF + NB + HB, :] = high[HB * x:HB * x + HB, :]
        lo = NB * HB + HL * x
        label[x, OFF - HL:OFF, :] = low[lo:lo + HL, :]
        label[x, OFF + NB:OFF + NB + HL, :] = high[lo:lo + HL, :]
    up[0:HB] = field[NB - HB:NB]
    up[HB:HB + HL] = label[NB - HL:NB]
    down[0:HB] = field[0:HB]
    down[HB:HB + HL] = label[0:HL]


def spread(couplings, z_ref, x):
    west, east, south, north, below, above = couplings
    here = z_ref[x]
    return (
        (west[x] * z_ref[x - 1] + east[x] * z_ref[x + 1])
        + (south[x] * pltpu.roll(here, 1, 0) + north[x] * pltpu.roll(here, YE - 1, 0))
        + (below[x] * pltpu.roll(here, 1, 1) + above[x] * pltpu.roll(here, NZ - 1, 1))
    )


def composite(couplings, t_ref, z_ref, u_ref, next_ref, halo):
    def first(x, _):
        z_ref[x] = ZT * t_ref[x] + ZS * spread(couplings, t_ref, x)
        return 0

    def second(x, _):
        u_ref[x] = UZ * z_ref[x] + UT * t_ref[x] + US * spread(couplings, z_ref, x)
        return 0

    def third(x, _):
        next_ref[x] = (t_ref[x] - u_ref[x]) + spread(couplings, u_ref, x)
        return 0

    for step, rows in ((first, halo + 2), (second, halo + 1), (third, halo)):
        lax.fori_loop(HL - rows, HL + NB + rows, step, 0)


def main_kernel(table, field, label, low, high, west, east, south, north, below, above,
                t0, t1, t2, u0, u1, diag, sums, half, z_ref):
    lining = 0.5 / table[0]
    first_kind = 0.5 / table[1]
    second_kind = 0.5 / table[2]
    third_kind = 0.5 / table[3]

    def kind(labels):
        return jnp.where(labels == 1.0, first_kind, jnp.where(
            labels == 2.0, second_kind, jnp.where(labels == 3.0, third_kind, lining)))

    def fetch_own(x, _):
        half[x + HL] = label[x]
        t0[x + HL] = field[x]
        return 0

    def fetch_low(x, _):
        half[x] = low[x + HB]
        half[x + HL + NB] = high[x + HB]
        return 0

    def fetch_field(x, _):
        t0[x + 1] = low[x]
        t0[x + HL + NB] = high[x]
        return 0

    lax.fori_loop(0, NB, fetch_own, 0)
    lax.fori_loop(0, HL, fetch_low, 0)
    lax.fori_loop(0, HB, fetch_field, 0)

    lane = lax.broadcasted_iota(jnp.int32, (YE, NZ), 1)
    at_low = lane == 0
    at_high = lane == NZ - 1

    def couple(x, carry):
        to_west, here = carry
        labels = half[x]
        inside = labels > 0.0
        beyond = kind(half[x + 1])
        to_east = 1.0 / (here + beyond)
        to_north = 1.0 / (here + pltpu.roll(here, YE - 1, 0))
        to_south = pltpu.roll(to_north, 1, 0)
        to_up = 1.0 / (here + jnp.where(at_high, lining, pltpu.roll(here, NZ - 1, 1)))
        to_down = jnp.where(at_low, 1.0 / (here + lining), pltpu.roll(to_up, 1, 1))
        whole = to_west + to_east + to_south + to_north + to_down + to_up
        inverse = jnp.where(inside, 1.0 / whole, 0.0)
        west[x] = to_west * inverse
        east[x] = to_east * inverse
        south[x] = to_south * inverse
        north[x] = to_north * inverse
        below[x] = jnp.where(at_low, 0.0, to_down * inverse)
        above[x] = jnp.where(at_high, 0.0, to_up * inverse)
        t0[x] = t0[x] * inverse
        diag[x] = whole
        return to_east, beyond

    here = kind(half[1])
    lax.fori_loop(1, XE - 1, couple, (1.0 / (kind(half[0]) + here), here))

    couplings = (west, east, south, north, below, above)
    composite(couplings, t0, z_ref, u0, t1, 6)
    composite(couplings, t1, z_ref, u1, t2, 3)

    row = lax.broadcasted_iota(jnp.int32, (YE, NZ), 0)
    own = (row >= OFF) & (row < OFF + NB)

    def dots(x, carry):
        s0, s1, s2, s3 = carry
        du0 = jnp.where(own, diag[x] * u0[x], 0.0)
        du1 = jnp.where(own, diag[x] * u1[x], 0.0)
        return (s0 + t0[x] * du0, s1 + t1[x] * du0, s2 + t1[x] * du1, s3 + t2[x] * du1)

    zero = jnp.zeros((YE, NZ), f32)
    parts = lax.fori_loop(HL, HL + NB, dots, (zero, zero, zero, zero))
    place = lax.broadcasted_iota(jnp.int32, (8, 128), 1)
    line = jnp.zeros((8, 128), f32)
    for k, part in enumerate(parts):
        line = jnp.where(place == k, jnp.sum(part), line)
    sums[...] = line


def last_kernel(west, east, south, north, below, above, t2, u2, t3, z_ref, w_ref):
    composite((west, east, south, north, below, above), t2, z_ref, w_ref, t3, 0)

    def keep(x, _):
        u2[x] = w_ref[x]
        return 0

    lax.fori_loop(HL, HL + NB, keep, 0)


CHUNK = 4


def final_kernel(sums, t0, t1, t2, t3, u0, u1, u2, diag, solution_out, residual_out, pre_out,
                 image_out, bufs, sems):
    total = jnp.sum(sums[...], axis=0, keepdims=True)
    m0, m1, m2, m3 = (total[0:1, k:k + 1] for k in range(4))
    curvature = m0 - m1
    step_one = m0 / curvature
    off_one = -m1 / curvature
    energy = off_one * off_one * m0 + 2.0 * off_one * step_one * m1 + step_one * step_one * m2
    bend = (off_one * off_one * (m0 - m1) + 2.0 * off_one * step_one * (m1 - m2)
            + step_one * step_one * (m2 - m3))
    momentum = energy / m0
    step_two = energy / (bend - momentum * energy / step_one)
    c2 = step_one * step_two
    c1 = step_one + step_two * (1.0 + momentum) - 2.0 * c2
    c0 = off_one * (1.0 - step_two) - step_two * momentum
    s0 = c1 + c2
    outs = (solution_out, residual_out, pre_out, image_out)
    copies = []
    for chunk in range(NB // CHUNK):
        def body(k, _):
            x = chunk * CHUNK + k
            e = x + HL
            own = (e, slice(OFF, OFF + NB))
            v0, v1, v2, v3 = t0[e], t1[e], t2[e], t3[e]
            w0, w1, w2 = u0[e], u1[e], u2[e]
            d = diag[e]
            part = slice(OFF, OFF + NB)
            bufs[0, x] = (s0 * w0 + c2 * w1)[part]
            bufs[1, x] = (d * (c0 * v0 + c1 * v1 + c2 * v2))[part]
            bufs[2, x] = (c0 * w0 + c1 * w1 + c2 * w2)[part]
            bufs[3, x] = (d * (c0 * (v0 - v1) + c1 * (v1 - v2) + c2 * (v2 - v3)))[part]
            return 0
        lax.fori_loop(0, CHUNK, body, 0)
        rows = slice(chunk * CHUNK, (chunk + 1) * CHUNK)
        for k in range(4):
            copy = pltpu.make_async_copy(bufs.at[k, rows], outs[k].at[rows], sems.at[chunk, k])
            copy.start()
            copies.append(copy)
    for copy in copies:
        copy.wait()


def neighbours(axis):
    count = lax.axis_size(axis)
    forward = [(i, i + 1) for i in range(count - 1)]
    return forward, [(target, source) for source, target in forward]


def swap(up, down, axis):
    forward, backward = neighbours(axis)
    return lax.ppermute(up, axis, forward), lax.ppermute(down, axis, backward)


def local(right_side, phase, table):
    up, down = pl.pallas_call(
        pack_kernel, name="pack", in_specs=[VM] * 2, out_specs=[VM] * 2,
        out_shape=[shape(NB * (HB + HL), NZ)] * 2, compiler_params=params(),
    )(right_side, phase)
    low, high = swap(up, down, "gy")
    field, label, up, down = pl.pallas_call(
        join_kernel, name="join", in_specs=[VM] * 4, out_specs=[VM] * 4,
        out_shape=[shape(NB, YE, NZ)] * 2 + [shape(HB + HL, YE, NZ)] * 2,
        compiler_params=params(),
    )(right_side, phase, low, high)
    low, high = swap(up, down, "gx")
    ext = shape(XE, YE, NZ)
    scratch = pltpu.VMEM((XE, YE, NZ), f32)
    *couplings, t0, t1, t2, u0, u1, diag, sums = pl.pallas_call(
        main_kernel, name="main", in_specs=[SM] + [VM] * 4, out_specs=[VM] * 13,
        out_shape=[ext] * 12 + [shape(8, 128)],
        scratch_shapes=[scratch, scratch], compiler_params=params(),
    )(table, field, label, low, high)
    across = lax.all_to_all(sums, "gx", 0, 0, tiled=True)
    across = jnp.broadcast_to(jnp.sum(across, 0, keepdims=True), (16, 128))
    gathered = lax.all_to_all(across, "gy", 0, 0, tiled=True)
    u2, t3 = pl.pallas_call(
        last_kernel, name="last", in_specs=[VM] * 7, out_specs=[VM] * 2,
        out_shape=[ext] * 2, scratch_shapes=[scratch, scratch], compiler_params=params(),
        cost_estimate=pl.CostEstimate(flops=20000000, bytes_accessed=12000000, transcendentals=0),
    )(*couplings, t2)
    brick = shape(NB, NB, NZ)
    hbm = pl.BlockSpec(memory_space=pl.ANY)
    return pl.pallas_call(
        final_kernel, name="final", in_specs=[VM] * 9, out_specs=[hbm] * 4,
        out_shape=[brick] * 4,
        scratch_shapes=[pltpu.VMEM((4, NB, NB, NZ), f32),
                        pltpu.SemaphoreType.DMA((NB // CHUNK, 4))],
        compiler_params=params(),
    )(gathered, t0, t1, t2, t3, u0, u1, u2, diag)


def solution(mesh):
    placed = (P("gx", "gy", None), P("gx", "gy", None), P())
    return jax.shard_map(
        local,
        mesh=mesh,
        in_specs=placed,
        out_specs=(P("gx", "gy", None),) * 4,
        check_vma=False,
    )
```

time: 361 us -> 160 us (0.44)
  blocking collectives: 136 us -> 8.81 us
  Pallas kernels: 0 us -> 95.6 us
  starting transfers between devices: 99.6 us -> 21.4 us
  other arithmetic: 56.1 us -> 0.03 us
  waiting for transfers between devices: 57 us -> 30.3 us
  between operations: 7.42 us -> 0.68 us
    psum x2 -> x0, blocking collectives: 136 us -> none  [local(): lax.psum((jnp.sum(residual * pre_residual), jnp.sum(residual_image * pre_...]
    pallas_call x0 -> x5, Pallas kernels: none -> 95.6 us  [the longest x1 54 us: local(): pl.pallas_call(main_kernel, name='main', in_specs=[SM] + [VM] * 4, out_sp...]
    ppermute x40 -> x4, starting transfers between devices: 99.6 us -> 12.1 us  [swap(): return (lax.ppermute(up, axis, forward), lax.ppermute(down, axis, backward))]
    ppermute x40 -> x4, waiting for transfers between devices: 57 us -> 30.3 us  [swap(): return (lax.ppermute(up, axis, forward), lax.ppermute(down, axis, backward))]
    add x5 -> x0, other arithmetic: 14.4 us -> none  [the longest x3 8.92 us: composite(): second = first + change]
    sub x3 -> x0, other arithmetic: 12.7 us -> none  [the longest x1 7.26 us: local(): pre_residual = pre_residual - step_size * pre_dir]
    concatenate x10 -> x0, other arithmetic: 11.3 us -> none  [extended(): block = jnp.concatenate([low, block, high], axis=dim)]
    mul x3 -> x0, other arithmetic: 9.5 us -> none  [composite(): first = start_scale * (vector / diagonal)]
  transfers between devices with their start and end apart: 40 -> 5, of which waited for: 18 -> 4; matrix products, arithmetic and copies ran while one was open for 1% -> 0% of each run, Pallas kernels for 0% -> 13%
where the time goes in v1:
time: 160 us
  Pallas kernels  95.6 us (60%)
  waiting for transfers between devices  30.3 us (19%)
  starting transfers between devices  21.4 us (13%)
  blocking collectives  8.81 us (6%)
  local copies, waits for them, and re-layouts  3.02 us (2%)
    pallas_call x1, Pallas kernels, local(): pl.pallas_call(main_kernel, name='main', in_specs=[SM] + [VM] * 4, out_sp...  54 us
    ppermute x4, waiting for transfers between devices, swap(): return (lax.ppermute(up, axis, forward), lax.ppermute(down, axis, backward))  30.3 us
    pallas_call x1, Pallas kernels, local(): pl.pallas_call(last_kernel, name='last', in_specs=[VM] * 7, out_specs=[VM...  20.8 us
    pallas_call x1, Pallas kernels, local(): pl.pallas_call(final_kernel, name='final', in_specs=[VM] * 9, out_specs=[...  13.4 us
    ppermute x4, starting transfers between devices, swap(): return (lax.ppermute(up, axis, forward), lax.ppermute(down, axis, backward))  12.1 us
    all_to_all x1, starting transfers between devices, local(): gathered = lax.all_to_all(across, 'gy', 0, 0, tiled=True)  9.29 us
    all_to_all x1, blocking collectives, local(): across = lax.all_to_all(sums, 'gx', 0, 0, tiled=True)  8.81 us
    pallas_call x1, Pallas kernels, local(): pl.pallas_call(join_kernel, name='join', in_specs=[VM] * 4, out_specs=[VM...  4.72 us
  transfers between devices with their start and end apart: 5, of which 4 were waited for; matrix products, arithmetic and copies ran while one was open for 0% of the time, Pallas kernels for 13%

profile of v1, /device:TPU:1, one launch (start us, length us, event | category | flops | bytes accessed | tf_op | source)
XLA Modules:
  0.0 159.8 jit_solution(7900748036582436071)
XLA Ops:
  0.6 2.8 %pack.1 = (f32[608,256]{1,0:T(8,128)}, f32[608,256]{1,0:T(8,128)}) custom-call(f32[32,32,256]{2,1,0:T(8,128)} %rhs.3, s32[32,32,256]{2,1,0:T(8,128)} %phase.3), custom_call_target="tpu_custom_call" | custom-call | tf_op jit(solution)/shard_map/pack/pallas_call | solution.py:250
  3.4 4.0 %collective-permute-start = (f32[608,256]{1,0:T(8,128)}, f32[608,256]{1,0:T(8,128)S(1)}, u32[]{:S(2)}, u32[]{:S(2)}) collective-permute-start(f32[608,256]{1,0:T(8,128)} %get-tuple-element.25), channel_id=1, source_target_pairs={{0,1},{1,2},{2,3},{3,4},{4,5},{5,6},{6,7},{7,8},{8,9},{9,10},{10,1... | collective-permute-start | bytes 1867784 | tf_op jit(solution)/shard_map/ppermute | solution.py:246
  7.4 1.3 collective-permute-start.1
  8.7 11.7 %collective-permute-done.low = f32[608,256]{1,0:T(8,128)S(1)} collective-permute-done((f32[608,256]{1,0:T(8,128)}, f32[608,256]{1,0:T(8,128)S(1)}, u32[]{:S(2)}, u32[]{:S(2)}) %collective-permute-start) | collective-permute-done | bytes 622624 | tf_op jit(solution)/shard_map/ppermute | solution.py:246
  20.3 0.0 copy-start.2
  20.3 3.8 %collective-permute-done.1.high = f32[608,256]{1,0:T(8,128)S(1)} collective-permute-done((f32[608,256]{1,0:T(8,128)}, f32[608,256]{1,0:T(8,128)S(1)}, u32[]{:S(2)}, u32[]{:S(2)}) %collective-permute-start.1) | collective-permute-done | bytes 622624 | tf_op jit(solution)/shard_map/ppermute | solution.py:246
  24.1 0.0 copy-done.2
  24.1 0.0 copy-start.3
  24.1 0.8 copy-done.3
  24.9 4.7 %join.1 = (f32[32,56,256]{2,1,0:T(8,128)}, f32[32,56,256]{2,1,0:T(8,128)}, f32[19,56,256]{2,1,0:T(8,128)}, f32[19,56,256]{2,1,0:T(8,128)}) custom-call(f32[32,32,256]{2,1,0:T(8,128)} %rhs.3, s32[32,32,256]{2,1,0:T(8,128)} %phase.3, f32[608,256]{1,0:T(8,128)} %copy-done.2, f32[608,256]{1,0:T(8,128)} %copy-done.3), custom_call_target="tpu_custom_call" | custom-call | tf_op jit(solution)/shard_map/join/pallas_call | solution.py:255
  29.6 4.9 %collective-permute-start.2 = (f32[19,56,256]{2,1,0:T(8,128)}, f32[19,56,256]{2,1,0:T(8,128)S(1)}, u32[]{:S(2)}, u32[]{:S(2)}) collective-permute-start(f32[19,56,256]{2,1,0:T(8,128)} %get-tuple-element.29), channel_id=1, source_target_pairs={{0,16},{16,32},{32,48},{48,64},{64,80},{80,96},{96,112},{1,17},{17... | collective-permute-start | bytes 3268616 | tf_op jit(solution)/shard_map/ppermute | solution.py:246
  34.5 1.9 %collective-permute-start.3 = (f32[19,56,256]{2,1,0:T(8,128)}, f32[19,56,256]{2,1,0:T(8,128)S(1)}, u32[]{:S(2)}, u32[]{:S(2)}) collective-permute-start(f32[19,56,256]{2,1,0:T(8,128)} %get-tuple-element.30), channel_id=1, source_target_pairs={{16,0},{32,16},{48,32},{64,48},{80,64},{96,80},{112,96},{17,1},{33... | collective-permute-start | bytes 3268616 | tf_op jit(solution)/shard_map/ppermute | solution.py:246
  36.5 10.5 %collective-permute-done.2.low = f32[19,56,256]{2,1,0:T(8,128)S(1)} collective-permute-done((f32[19,56,256]{2,1,0:T(8,128)}, f32[19,56,256]{2,1,0:T(8,128)S(1)}, u32[]{:S(2)}, u32[]{:S(2)}) %collective-permute-start.2) | collective-permute-done | bytes 1089568 | tf_op jit(solution)/shard_map/ppermute | solution.py:246
  47.0 0.0 copy-start
  47.0 4.3 %collective-permute-done.3.high = f32[19,56,256]{2,1,0:T(8,128)S(1)} collective-permute-done((f32[19,56,256]{2,1,0:T(8,128)}, f32[19,56,256]{2,1,0:T(8,128)S(1)}, u32[]{:S(2)}, u32[]{:S(2)}) %collective-permute-start.3) | collective-permute-done | bytes 1089568 | tf_op jit(solution)/shard_map/ppermute | solution.py:246
  51.3 0.0 copy-start.1
  51.3 0.0 copy-done
  51.3 1.0 copy-done.1
  52.3 54.0 %main.1 = (f32[52,56,256]{2,1,0:T(8,128)}, f32[52,56,256]{2,1,0:T(8,128)}, f32[52,56,256]{2,1,0:T(8,128)}, f32[52,56,256]{2,1,0:T(8,128)}, f32[52,56,256]{2,1,0:...) custom-call(f32[4]{0:T(128)} %table.1, ...), custom_call_target="tpu_custom_call" | custom-call | tf_op jit(solution)/shard_map/main/pallas_call | solution.py:263
  106.3 8.8 %all_to_all.17 = f32[8,1,128]{2,1,0:T(1,128)S(1)} all-to-all(f32[8,1,128]{2,1,0:T(1,128)} %bitcast.5), channel_id=1, replica_groups=mesh['gx'=8,'gy'=16] {'gx'}, dimensions={0} | all-to-all | bytes 8192 | tf_op jit(solution)/shard_map/all_to_all | solution.py:268
  115.1 0.6 broadcast_in_dim.2
  115.7 9.3 %all-to-all-start.1 = ((f32[16,1,128]{2,1,0:T(1,128)}), f32[16,1,128]{2,1,0:T(1,128)S(1)}, u32[]{:S(2)}, u32[]{:S(2)}) async-start(f32[16,1,128]{2,1,0:T(1,128)} %broadcast_in_dim.2), calls=%async_computation.1 | async-start | bytes 16384 | tf_op jit(solution)/shard_map/all_to_all | solution.py:270
  125.0 20.8 %last.1 = (f32[52,56,256]{2,1,0:T(8,128)}, f32[52,56,256]{2,1,0:T(8,128)}) custom-call(f32[52,56,256]{2,1,0:T(8,128)} %get-tuple-element.35.west, f32[52,56,256]{2,1,0:T(8,128)} %get-tuple-element.36.east, f32[52,56,256]{2,1,0:T(8,128)} %get-tuple-element.37.south, f32[52,56,256]{2,1,0:T(8,128)} %get-tuple-element.38.north, ...), custom_call_target="tpu_custom_call" | custom-call | flops 20000000 | bytes 12000000 | tf_op jit(solution)/shard_map/last/pallas_call | solution.py:271
  145.8 0.0 all-to-all-done.1
  145.8 0.0 copy-start.4
  145.8 0.6 copy-done.4
  146.4 13.4 %final.1 = (f32[32,32,256]{2,1,0:T(8,128)}, f32[32,32,256]{2,1,0:T(8,128)}, f32[32,32,256]{2,1,0:T(8,128)}, f32[32,32,256]{2,1,0:T(8,128)}) custom-call(f32[16,128]{1,0:T(8,128)} %bitcast.4, f32[52,56,256]{2,1,0:T(8,128)} %get-tuple-element.32.t0, f32[52,56,256]{2,1,0:T(8,128)} %get-tuple-element.33.t1, f32[52,56,256]{2,1,0:T(8,128)} %get-tuple-element.34.t2, ...), custom_call_target="tpu_custom_call" | custom-call | tf_op jit(solution)/shard_map/final/pallas_call | solution.py:278
  (1 shorter events, 0.0 us)
Async XLA Ops:
  3.4 16.9 %collective-permute-start = (f32[608,256]{1,0:T(8,128)}, f32[608,256]{1,0:T(8,128)S(1)}, u32[]{:S(2)}, u32[]{:S(2)}) collective-permute-start(f32[608,256]{1,0:T(8,128)} %get-tuple-element.25), channel_id=1, source_target_pairs={{0,1},{1,2},{2,3},{3,4},{4,5},{5,6},{6,7},{7,8},{8,9},{9,10},{10,1... | collective-permute-start | bytes 1867784 | tf_op jit(solution)/shard_map/ppermute | solution.py:246
  7.4 16.7 %collective-permute-start.1 = (f32[608,256]{1,0:T(8,128)}, f32[608,256]{1,0:T(8,128)S(1)}, u32[]{:S(2)}, u32[]{:S(2)}) collective-permute-start(f32[608,256]{1,0:T(8,128)} %get-tuple-element.26), channel_id=1, source_target_pairs={{1,0},{2,1},{3,2},{4,3},{5,4},{6,5},{7,6},{8,7},{9,8},{10,9},{11,1... | collective-permute-start | bytes 1867784 | tf_op jit(solution)/shard_map/ppermute | solution.py:246
  20.3 3.8 %copy-start.2 = (f32[608,256]{1,0:T(8,128)}, f32[608,256]{1,0:T(8,128)S(1)}, u32[]{:S(2)}) copy-start(f32[608,256]{1,0:T(8,128)S(1)} %collective-permute-done.low) | copy-start | bytes 1867780
  24.1 0.8 copy-start.3
  29.6 17.4 %collective-permute-start.2 = (f32[19,56,256]{2,1,0:T(8,128)}, f32[19,56,256]{2,1,0:T(8,128)S(1)}, u32[]{:S(2)}, u32[]{:S(2)}) collective-permute-start(f32[19,56,256]{2,1,0:T(8,128)} %get-tuple-element.29), channel_id=1, source_target_pairs={{0,16},{16,32},{32,48},{48,64},{64,80},{80,96},{96,112},{1,17},{17... | collective-permute-start | bytes 3268616 | tf_op jit(solution)/shard_map/ppermute | solution.py:246
  34.5 16.8 %collective-permute-start.3 = (f32[19,56,256]{2,1,0:T(8,128)}, f32[19,56,256]{2,1,0:T(8,128)S(1)}, u32[]{:S(2)}, u32[]{:S(2)}) collective-permute-start(f32[19,56,256]{2,1,0:T(8,128)} %get-tuple-element.30), channel_id=1, source_target_pairs={{16,0},{32,16},{48,32},{64,48},{80,64},{96,80},{112,96},{17,1},{33... | collective-permute-start | bytes 3268616 | tf_op jit(solution)/shard_map/ppermute | solution.py:246
  47.0 4.3 %copy-start = (f32[19,56,256]{2,1,0:T(8,128)}, f32[19,56,256]{2,1,0:T(8,128)S(1)}, u32[]{:S(2)}) copy-start(f32[19,56,256]{2,1,0:T(8,128)S(1)} %collective-permute-done.2.low) | copy-start | bytes 3268612
  51.3 1.0 copy-start.1
  115.7 30.1 %all-to-all-start.1 = ((f32[16,1,128]{2,1,0:T(1,128)}), f32[16,1,128]{2,1,0:T(1,128)S(1)}, u32[]{:S(2)}, u32[]{:S(2)}) async-start(f32[16,1,128]{2,1,0:T(1,128)} %broadcast_in_dim.2), calls=%async_computation.1 | async-start | bytes 16384 | tf_op jit(solution)/shard_map/all_to_all | solution.py:270
  145.8 0.6 copy-start.4

commit v2 on v1

v2 whole, which is shorter than its diff:
```python
import jax
import jax.numpy as jnp
from jax import lax
from jax.experimental import pallas as pl
from jax.experimental.pallas import tpu as pltpu
from jax.sharding import PartitionSpec as P

centre_value = 1.1
half_width = 0.9
ratio_sigma = centre_value / half_width
rho_first = 1.0 / ratio_sigma
rho_second = 1.0 / (2.0 * ratio_sigma - rho_first)
rho_third = 1.0 / (2.0 * ratio_sigma - rho_second)
start_scale = 1.0 / centre_value
keep_first = rho_second * rho_first
push_first = 2.0 * rho_second / half_width
keep_second = rho_third * rho_second
push_second = 2.0 * rho_third / half_width

ZT = (1.0 + keep_first - push_first) * start_scale + push_first
ZS = push_first * start_scale
UZ = 1.0 + keep_second - push_second
UT = push_second - keep_second * start_scale
US = push_second

NB = 32
HB = 9
HL = 10
OFF = 12
YE = 56
XE = NB + 2 * HL
NZ = 256
VM = pl.BlockSpec(memory_space=pltpu.VMEM)
SM = pl.BlockSpec(memory_space=pltpu.SMEM)
f32 = jnp.float32


def shape(*dims):
    return jax.ShapeDtypeStruct(dims, f32)


def params(mib):
    return pltpu.CompilerParams(vmem_limit_bytes=mib * 1024 * 1024)

HALF = NZ // 2


def lanes(h):
    return slice(HALF * h, HALF * h + HALF)


def pack_kernel(rhs, phase, up, down):
    for x in range(NB):
        lo = NB * HB + HL * x
        for h in range(2):
            up[h, HB * x:HB * x + HB] = rhs[x, NB - HB:NB, lanes(h)]
            down[h, HB * x:HB * x + HB] = rhs[x, 0:HB, lanes(h)]
            up[h, lo:lo + HL] = phase[x, NB - HL:NB, lanes(h)].astype(f32)
            down[h, lo:lo + HL] = phase[x, 0:HL, lanes(h)].astype(f32)


def join_kernel(rhs, phase, low, high, field, label, up, down):
    edge = jnp.zeros((2, OFF - HL, HALF), f32)
    for x in range(NB):
        lo = NB * HB + HL * x
        for ref, width, base in ((field, HB, HB * x), (label, HL, lo)):
            own = rhs[x] if ref is field else phase[x].astype(f32)
            ref[x, :, 0:8] = jnp.zeros((2, 8, HALF), f32)
            ref[x, :, YE - 8:YE] = jnp.zeros((2, 8, HALF), f32)
            for h in range(2):
                ref[x, h, OFF:OFF + NB] = own[:, lanes(h)]
                ref[x, h, OFF - width:OFF] = low[h, base:base + width]
                ref[x, h, OFF + NB:OFF + NB + width] = high[h, base:base + width]
    up[0:HB] = field[NB - HB:NB]
    up[HB:HB + HL] = label[NB - HL:NB]
    down[0:HB] = field[0:HB]
    down[HB:HB + HL] = label[0:HL]


def machine(table, label_at, field_at, arrays):
    west, east, south, north, below, above, diag, t, z, u = arrays
    lining = 0.5 / table[0]
    first_kind = 0.5 / table[1]
    second_kind = 0.5 / table[2]
    third_kind = 0.5 / table[3]
    lane = lax.broadcasted_iota(jnp.int32, (YE, HALF), 1)
    at_low = lane == 0
    at_high = lane == HALF - 1
    real = slice(8, 8 + YE)

    def kind(labels):
        return jnp.where(labels == 1.0, first_kind, jnp.where(
            labels == 2.0, second_kind, jnp.where(labels == 3.0, third_kind, lining)))

    def clear(refs):
        def body(x, _):
            for ref in refs:
                ref[x, :, 0:8] = jnp.zeros((2, 8, HALF), f32)
                ref[x, :, 8 + YE:16 + YE] = jnp.zeros((2, 8, HALF), f32)
            return 0
        lax.fori_loop(0, XE, body, 0)

    def couple(start, stop):
        def body(x, carry):
            to_west, here = carry
            beyond = tuple(kind(label_at(x + 1, h)) for h in range(2))
            to_east = tuple(1.0 / (here[h] + beyond[h]) for h in range(2))
            to_north = tuple(1.0 / (here[h] + pltpu.roll(here[h], YE - 1, 0)) for h in range(2))
            after = tuple(pltpu.roll(here[h], HALF - 1, 1) for h in range(2))
            to_up = (1.0 / (here[0] + jnp.where(at_high, after[1], after[0])),
                     1.0 / (here[1] + jnp.where(at_high, lining, after[1])))
            moved = tuple(pltpu.roll(to_up[h], 1, 1) for h in range(2))
            to_down = (jnp.where(at_low, 1.0 / (here[0] + lining), moved[0]),
                       jnp.where(at_low, moved[0], moved[1]))
            for h in range(2):
                to_south = pltpu.roll(to_north[h], 1, 0)
                whole = (to_west[h] + to_east[h] + to_south + to_north[h] + to_down[h] + to_up[h])
                inverse = jnp.where(label_at(x, h) > 0.0, 1.0 / whole, 0.0)
                west[x, h] = to_west[h] * inverse
                east[x, h] = to_east[h] * inverse
                south[x, h] = to_south * inverse
                north[x, h] = to_north[h] * inverse
                down = to_down[h] * inverse
                rise = to_up[h] * inverse
                below[x, h] = jnp.where(at_low, 0.0, down) if h == 0 else down
                above[x, h] = jnp.where(at_high, 0.0, rise) if h == 1 else rise
                t[x, h, real] = field_at(x, h) * inverse
                diag[x, h] = whole
            return to_east, beyond

        here = tuple(kind(label_at(start, h)) for h in range(2))
        to_west = tuple(1.0 / (kind(label_at(start - 1, h)) + here[h]) for h in range(2))
        lax.fori_loop(start, stop, body, (to_west, here))

    def spread(ref, x, finish):
        here = tuple(ref[x, h, real] for h in range(2))
        back = tuple(pltpu.roll(here[h], 1, 1) for h in range(2))
        ahead = tuple(pltpu.roll(here[h], HALF - 1, 1) for h in range(2))
        lower = (back[0], jnp.where(at_low, back[0], back[1]))
        upper = (jnp.where(at_high, ahead[1], ahead[0]), ahead[1])
        for h in range(2):
            total = (
                (west[x, h] * ref[x - 1, h, real] + east[x, h] * ref[x + 1, h, real])
                + (south[x, h] * ref[x, h, 7:7 + YE] + north[x, h] * ref[x, h, 9:9 + YE])
                + (below[x, h] * lower[h] + above[x, h] * upper[h])
            )
            finish(h, here[h], total)

    def first(x, _):
        def finish(h, here, total):
            z[x, h, real] = ZT * here + ZS * total
        spread(t, x, finish)
        return 0

    def second(x, _):
        def finish(h, here, total):
            u[x, h, real] = UZ * here + UT * t[x, h, real] + US * total
        spread(z, x, finish)
        return 0

    def third(x, _):
        def finish(h, here, total):
            t[x, h, real] = (t[x, h, real] - here) + total
        spread(u, x, finish)
        return 0

    def run(stage, ranges):
        for start, stop in ranges:
            size = stop - start
            unroll = 4 if size % 4 == 0 else 3 if size % 3 == 0 else 2 if size % 2 == 0 else 1
            lax.fori_loop(start, stop, (first, second, third)[stage % 3], 0,
                          unroll=unroll if size > unroll else True)

    def run_sides(stage, low, high, size):
        step = (first, second, third)[stage % 3]

        def body(i, _):
            step(low + i, 0)
            step(high + i, 0)
            return 0
        lax.fori_loop(0, size, body, 0, unroll=2)

    def keep(ranges, u_out, r_out, pairs):
        own = slice(8 + OFF, 8 + OFF + NB)
        zero = jnp.zeros((NB, HALF), f32)

        def body(x, carry):
            totals = list(carry)
            for h in range(2):
                pre = u[x, h, own]
                res = t[x, h, own] * diag[x, h, OFF:OFF + NB]
                u_out[x - HL, :, lanes(h)] = pre
                r_out[x - HL, :, lanes(h)] = res
                for k, other in enumerate(pairs):
                    left = res if other is None else other[x - HL, :, lanes(h)]
                    totals[k] = totals[k] + left * pre
            return tuple(totals)

        totals = (zero,) * len(pairs)
        for start, stop in ranges:
            totals = lax.fori_loop(start, stop, body, totals)
        return totals

    return clear, couple, run, run_sides, keep


def as_line(parts):
    place = lax.broadcasted_iota(jnp.int32, (8, 128), 1)
    line = jnp.zeros((8, 128), f32)
    for k, part in enumerate(parts):
        line = jnp.where(place == k, jnp.sum(part), line)
    return line


LO, HI = HL, HL + NB
SUM_OF = ((None,), (None,), ())


def inner_kernel(table, rhs, field, label, *refs):
    arrays, kept, sums = refs[:10], refs[10:16], refs[16]
    r1, r2, r3, u0, u1, u2 = kept
    clear, couple, run, _, keep = machine(
        table, lambda x, h: label[x - HL, h], lambda x, h: field[x - HL, h], arrays)
    clear(arrays[7:])
    couple(LO + 1, HI - 1)
    parts = ()
    for stage in range(9):
        run(stage, ((LO + 2 + stage, HI - 2 - stage),))
        if stage == 2:
            parts += keep(((LO + 2 + stage, HI - 2 - stage),), u0, r1, (rhs, None))
        if stage == 5:
            parts += keep(((LO + 2 + stage, HI - 2 - stage),), u1, r2, (r1, None))
        if stage == 8:
            keep(((LO + 2 + stage, HI - 2 - stage),), u2, r3, ())
    sums[...] = as_line(parts)


def outer_kernel(table, rhs, field, label, low, high, part_sums, *refs):
    arrays, kept, sums, labels = refs[16:26], refs[26:32], refs[32], refs[33]
    r1, r2, r3, u0, u1, u2 = kept
    t = arrays[8]
    for x in range(HL):
        labels[0, x] = low[HB + x]
        labels[1, x + 2] = high[HB + x]
    for x in range(2):
        labels[0, HL + x] = label[x]
        labels[1, x] = label[NB - 2 + x]
    t[LO, :, 8:8 + YE] = field[0]
    t[HI - 1, :, 8:8 + YE] = field[NB - 1]
    for x in range(HB):
        t[LO - HB + x, :, 8:8 + YE] = low[x]
        t[HI + x, :, 8:8 + YE] = high[x]

    def field_at(x, h):
        return t[x, h, 8:8 + YE]

    for side, base, start in ((0, 0, 1), (1, HI - 2, HI - 1)):
        couple = machine(table, lambda x, h: labels[side, x - base, h], field_at, arrays)[1]
        couple(start, start + HL)
    _, _, _, run_sides, keep = machine(table, None, None, arrays)
    parts = ()
    for stage in range(9):
        run_sides(stage, 2 + stage, HI - 2 - stage, HL)
        rest = ((LO, LO + 2 + stage), (HI - 2 - stage, HI))
        if stage == 2:
            parts += keep(rest, u0, r1, (rhs, None))
        if stage == 5:
            parts += keep(rest, u1, r2, (r1, None))
        if stage == 8:
            keep(rest, u2, r3, ())
    sums[...] = part_sums[...] + as_line(parts)


INNER, OUTER = 2, 4
CHUNK = 4


def final_kernel(sums, r0, r1, r2, r3, u0, u1, u2, solution_out, residual_out, pre_out,
                 image_out, bufs, sems):
    total = jnp.sum(sums[...], axis=0, keepdims=True)
    m0, m1, m2, m3 = (total[0:1, k:k + 1] for k in range(4))
    curvature = m0 - m1
    step_one = m0 / curvature
    off_one = -m1 / curvature
    energy = off_one * off_one * m0 + 2.0 * off_one * step_one * m1 + step_one * step_one * m2
    bend = (off_one * off_one * (m0 - m1) + 2.0 * off_one * step_one * (m1 - m2)
            + step_one * step_one * (m2 - m3))
    momentum = energy / m0
    step_two = energy / (bend - momentum * energy / step_one)
    c2 = step_one * step_two
    c1 = step_one + step_two * (1.0 + momentum) - 2.0 * c2
    c0 = off_one * (1.0 - step_two) - step_two * momentum
    s0 = c1 + c2
    outs = (solution_out, residual_out, pre_out, image_out)
    copies = []
    for chunk in range(NB // CHUNK):
        def body(k, _):
            x = chunk * CHUNK + k
            v0, v1, v2, v3 = r0[x], r1[x], r2[x], r3[x]
            w0, w1, w2 = u0[x], u1[x], u2[x]
            bufs[0, x] = s0 * w0 + c2 * w1
            bufs[1, x] = c0 * v0 + c1 * v1 + c2 * v2
            bufs[2, x] = c0 * w0 + c1 * w1 + c2 * w2
            bufs[3, x] = c0 * (v0 - v1) + c1 * (v1 - v2) + c2 * (v2 - v3)
            return 0
        lax.fori_loop(0, CHUNK, body, 0)
        rows = slice(chunk * CHUNK, (chunk + 1) * CHUNK)
        for k in range(4):
            copy = pltpu.make_async_copy(bufs.at[k, rows], outs[k].at[rows], sems.at[chunk, k])
            copy.start()
            copies.append(copy)
    for copy in copies:
        copy.wait()


def neighbours(axis):
    count = lax.axis_size(axis)
    forward = [(i, i + 1) for i in range(count - 1)]
    return forward, [(target, source) for source, target in forward]


def swap(up, down, axis):
    forward, backward = neighbours(axis)
    return lax.ppermute(up, axis, forward), lax.ppermute(down, axis, backward)


def local(right_side, phase, table):
    up, down = pl.pallas_call(
        pack_kernel, name="pack", in_specs=[VM] * 2, out_specs=[VM] * 2,
        out_shape=[shape(2, NB * (HB + HL), HALF)] * 2, compiler_params=params(4),
    )(right_side, phase)
    low, high = swap(up, down, "gy")
    field, label, up, down = pl.pallas_call(
        join_kernel, name="join", in_specs=[VM] * 4, out_specs=[VM] * 4,
        out_shape=[shape(NB, 2, YE, HALF)] * 2 + [shape(HB + HL, 2, YE, HALF)] * 2,
        compiler_params=params(14),
    )(right_side, phase, low, high)
    low, high = swap(up, down, "gx")
    brick = shape(NB, NB, NZ)
    state = [shape(XE, 2, YE, HALF)] * 7 + [shape(XE, 2, YE + 16, HALF)] * 3 + [brick] * 6
    *kept, sums = pl.pallas_call(
        inner_kernel, name="inner", in_specs=[SM] + [VM] * 3, out_specs=[VM] * 17,
        out_shape=state + [shape(8, 128)], compiler_params=params(INNER),
        cost_estimate=pl.CostEstimate(flops=30000000, bytes_accessed=30000000, transcendentals=0),
    )(table, right_side, field, label)
    *kept, sums = pl.pallas_call(
        outer_kernel, name="outer", in_specs=[SM] + [VM] * 22, out_specs=[VM] * 17,
        out_shape=state + [shape(8, 128)], compiler_params=params(OUTER),
        scratch_shapes=[pltpu.VMEM((2, HL + 2, 2, YE, HALF), f32)],
        input_output_aliases={7 + k: k for k in range(16)},
    )(table, right_side, field, label, low, high, sums, *kept)
    kept = kept[10:]
    gathered = lax.all_to_all(
        jnp.broadcast_to(sums[0:1], (128, 128)), ("gx", "gy"), 0, 0, tiled=True)
    hbm = pl.BlockSpec(memory_space=pl.ANY)
    return pl.pallas_call(
        final_kernel, name="final", in_specs=[VM] * 8, out_specs=[hbm] * 4,
        out_shape=[brick] * 4,
        scratch_shapes=[pltpu.VMEM((4, NB, NB, NZ), f32),
                        pltpu.SemaphoreType.DMA((NB // CHUNK, 4))],
        compiler_params=params(14),
    )(gathered, right_side, *kept)


def solution(mesh):
    placed = (P("gx", "gy", None), P("gx", "gy", None), P())
    return jax.shard_map(
        local,
        mesh=mesh,
        in_specs=placed,
        out_specs=(P("gx", "gy", None),) * 4,
        check_vma=False,
    )
```

time: 160 us -> 101 us (0.63)
  Pallas kernels: 95.6 us -> 45.2 us
  waiting for transfers between devices: 30.3 us -> 15.2 us
  blocking collectives: 8.81 us -> 21.9 us
  starting transfers between devices: 21.4 us -> 12.2 us
  local copies, waits for them, and re-layouts: 3.02 us -> 4.94 us
    pallas_call x3, Pallas kernels: 88.2 us -> 44.5 us  [the longest x1 21.4 us: local(): pl.pallas_call(inner_kernel, name='inner', in_specs=[SM] + [VM] * 3, out_...]
    ppermute x4, waiting for transfers between devices: 30.3 us -> 15.2 us  [swap(): return (lax.ppermute(up, axis, forward), lax.ppermute(down, axis, backward))]
    all_to_all x1, blocking collectives: 8.81 us -> 21.9 us  [local(): lax.all_to_all(jnp.broadcast_to(sums[0:1], (128, 128)), ('gx', 'gy'), 0,...]
    all_to_all x1 -> x0, starting transfers between devices: 9.29 us -> none  [local(): gathered = lax.all_to_all(across, 'gy', 0, 0, tiled=True)]
    pallas_call x1, Pallas kernels: 4.72 us -> 0.48 us  [local(): pl.pallas_call(join_kernel, name='join', in_specs=[VM] * 4, out_specs=[VM...]
    pallas_call x1, Pallas kernels: 2.76 us -> 0.14 us  [local(): pl.pallas_call(pack_kernel, name='pack', in_specs=[VM] * 2, out_specs=[VM...]
    unnamed x10 -> x12, local copies, waits for them, and re-layouts: 2.42 us -> 4.9 us
  transfers between devices with their start and end apart: 5 -> 4, of which waited for: 4 -> 2; matrix products, arithmetic and copies ran while one was open for 0% -> 0% of each run, Pallas kernels for 13% -> 21%
where the time goes in v2:
time: 101 us; the launch traced here: 100 us
  Pallas kernels  45.2 us (45%)
  blocking collectives  21.9 us (22%)
  waiting for transfers between devices  15.2 us (15%)
  starting transfers between devices  12.2 us (12%)
  local copies, waits for them, and re-layouts  4.94 us (5%)
    all_to_all x1, blocking collectives, local(): lax.all_to_all(jnp.broadcast_to(sums[0:1], (128, 128)), ('gx', 'gy'), 0,...  21.9 us
    pallas_call x1, Pallas kernels, local(): pl.pallas_call(inner_kernel, name='inner', in_specs=[SM] + [VM] * 3, out_...  21.4 us
    pallas_call x1, Pallas kernels, local(): pl.pallas_call(outer_kernel, name='outer', in_specs=[SM] + [VM] * 22, out...  18.1 us
    ppermute x4, waiting for transfers between devices, swap(): return (lax.ppermute(up, axis, forward), lax.ppermute(down, axis, backward))  15.2 us
    ppermute x4, starting transfers between devices, swap(): return (lax.ppermute(up, axis, forward), lax.ppermute(down, axis, backward))  12.2 us
    pallas_call x1, Pallas kernels, local(): pl.pallas_call(final_kernel, name='final', in_specs=[VM] * 8, out_specs=[...  5.1 us
    unnamed x12, local copies, waits for them, and re-layouts  4.9 us
  transfers between devices with their start and end apart: 4, of which 2 were waited for; matrix products, arithmetic and copies ran while one was open for 0% of the time, Pallas kernels for 21%

profile of v2, /device:TPU:1, one launch (start us, length us, event | category | flops | bytes accessed | tf_op | source)
XLA Modules:
  0.0 100.2 jit_solution(2839409716247185461)
XLA Ops:
  0.6 0.0 copy-start
  0.6 1.2 %copy-done = f32[32,32,256]{2,1,0:T(8,128)S(1)} copy-done((f32[32,32,256]{2,1,0:T(8,128)S(1)}, f32[32,32,256]{2,1,0:T(8,128)}, u32[]{:S(2)}) %copy-start) | copy-done | bytes 1048600
  1.9 0.0 copy-start.3
  1.9 1.2 %copy-done.3 = s32[32,32,256]{2,1,0:T(8,128)S(1)} copy-done((s32[32,32,256]{2,1,0:T(8,128)S(1)}, s32[32,32,256]{2,1,0:T(8,128)}, u32[]{:S(2)}) %copy-start.3) | copy-done | bytes 1048600
  3.1 0.0 copy-start.2
  3.1 0.0 copy-start.5
  3.1 0.1 pack.1
  3.2 4.1 %collective-permute-start = (f32[2,608,128]{2,1,0:T(8,128)S(1)}, f32[2,608,128]{2,1,0:T(8,128)S(1)}, u32[]{:S(2)}, u32[]{:S(2)}) collective-permute-start(f32[2,608,128]{2,1,0:T(8,128)S(1)} %get-tuple-element.34), channel_id=1, source_target_pairs={{0,1},{1,2},{2,3},{3,4},{4,5},{5,6},{6,7},{7,8},{8,9},{9,10},{10,1... | collective-permute-start | bytes 1867784 | tf_op jit(solution)/shard_map/ppermute | solution.py:324
  7.3 1.3 %collective-permute-start.1 = (f32[2,608,128]{2,1,0:T(8,128)S(1)}, f32[2,608,128]{2,1,0:T(8,128)S(1)}, u32[]{:S(2)}, u32[]{:S(2)}) collective-permute-start(f32[2,608,128]{2,1,0:T(8,128)S(1)} %get-tuple-element.35), channel_id=1, source_target_pairs={{1,0},{2,1},{3,2},{4,3},{5,4},{6,5},{7,6},{8,7},{9,8},{10,9},{11,1... | collective-permute-start | bytes 1867784 | tf_op jit(solution)/shard_map/ppermute | solution.py:324
  8.6 11.4 %collective-permute-done.low = f32[2,608,128]{2,1,0:T(8,128)S(1)} collective-permute-done((f32[2,608,128]{2,1,0:T(8,128)S(1)}, f32[2,608,128]{2,1,0:T(8,128)S(1)}, u32[]{:S(2)}, u32[]{:S(2)}) %collective-permute-start) | collective-permute-done | bytes 622624 | tf_op jit(solution)/shard_map/ppermute | solution.py:324
  20.0 3.9 %collective-permute-done.1.high = f32[2,608,128]{2,1,0:T(8,128)S(1)} collective-permute-done((f32[2,608,128]{2,1,0:T(8,128)S(1)}, f32[2,608,128]{2,1,0:T(8,128)S(1)}, u32[]{:S(2)}, u32[]{:S(2)}) %collective-permute-start.1) | collective-permute-done | bytes 622624 | tf_op jit(solution)/shard_map/ppermute | solution.py:324
  23.9 0.0 copy-start.1
  23.9 1.2 %copy-done.1 = f32[32,32,256]{2,1,0:T(8,128)S(1)} copy-done((f32[32,32,256]{2,1,0:T(8,128)S(1)}, f32[32,32,256]{2,1,0:T(8,128)}, u32[]{:S(2)}) %copy-start.1) | copy-done | bytes 1048600
  25.1 0.0 copy-start.4
  25.1 1.2 %copy-done.4 = s32[32,32,256]{2,1,0:T(8,128)S(1)} copy-done((s32[32,32,256]{2,1,0:T(8,128)S(1)}, s32[32,32,256]{2,1,0:T(8,128)}, u32[]{:S(2)}) %copy-start.4) | copy-done | bytes 1048600
  26.3 0.5 join.1
  26.8 4.9 %collective-permute-start.2 = (f32[19,2,56,128]{3,2,1,0:T(8,128)S(1)}, f32[19,2,56,128]{3,2,1,0:T(8,128)S(1)}, u32[]{:S(2)}, u32[]{:S(2)}) collective-permute-start(f32[19,2,56,128]{3,2,1,0:T(8,128)S(1)} %get-tuple-element.38), channel_id=1, source_target_pairs={{0,16},{16,32},{32,48},{48,64},{64,80},{80,96},{96,112},{1,17},{17... | collective-permute-start | bytes 3268616 | tf_op jit(solution)/shard_map/ppermute | solution.py:324
  31.7 1.9 %collective-permute-start.3 = (f32[19,2,56,128]{3,2,1,0:T(8,128)S(1)}, f32[19,2,56,128]{3,2,1,0:T(8,128)S(1)}, u32[]{:S(2)}, u32[]{:S(2)}) collective-permute-start(f32[19,2,56,128]{3,2,1,0:T(8,128)S(1)} %get-tuple-element.39), channel_id=1, source_target_pairs={{16,0},{32,16},{48,32},{64,48},{80,64},{96,80},{112,96},{17,1},{33... | collective-permute-start | bytes 3268616 | tf_op jit(solution)/shard_map/ppermute | solution.py:324
  33.6 0.0 copy-done.2
  33.6 0.0 copy-done.5
  33.7 21.4 %inner.1 = (f32[52,2,56,128]{3,2,1,0:T(8,128)S(1)}, f32[52,2,56,128]{3,2,1,0:T(8,128)S(1)}, f32[52,2,56,128]{3,2,1,0:T(8,128)S(1)}, f32[52,2,56,128]{3,2,1,0:T(8...) custom-call(f32[4]{0:T(128)S(1)} %copy-done.5, ...), custom_call_target="tpu_custom_call" | custom-call | flops 30000000 | bytes 30000000 | tf_op jit(solution)/shard_map/inner/pallas_call | solution.py:341
  55.0 0.0 collective-permute-done.2.low
  55.0 0.0 collective-permute-done.3.high
  55.0 18.1 %outer.1 = (f32[52,2,56,128]{3,2,1,0:T(8,128)S(1)}, f32[52,2,56,128]{3,2,1,0:T(8,128)S(1)}, f32[52,2,56,128]{3,2,1,0:T(8,128)S(1)}, f32[52,2,56,128]{3,2,1,0:T(8...) custom-call(f32[4]{0:T(128)S(1)} %copy-done.5, ...), custom_call_target="tpu_custom_call", output_to_operand_aliasing={{0}: (7, {}), {1}: (8, {}), {2}: (9, {}), {3}: (10, {}), {4... | custom-call | tf_op jit(solution)/shard_map/outer/pallas_call | solution.py:346
  73.2 21.9 %all_to_all.8 = f32[128,1,128]{2,1,0:T(1,128)S(1)} all-to-all(f32[128,1,128]{2,1,0:T(1,128)S(1)} %broadcast_in_dim.2), channel_id=1, replica_groups=mesh['gx'=8,'gy'=16] {'gx','gy'}, dimensions={0} | all-to-all | bytes 131072 | tf_op jit(solution)/shard_map/all_to_all | solution.py:353
  95.1 5.1 %final.1 = (f32[32,32,256]{2,1,0:T(8,128)}, f32[32,32,256]{2,1,0:T(8,128)}, f32[32,32,256]{2,1,0:T(8,128)}, f32[32,32,256]{2,1,0:T(8,128)}) custom-call(f32[128,128]{1,0:T(8,128)S(1)} %bitcast.3, f32[32,32,256]{2,1,0:T(8,128)S(1)} %copy-done.2, f32[32,32,256]{2,1,0:T(8,128)S(1)} %get-tuple-element.58.r1, f32[32,32,256]{2,1,0:T(8,128)S(1)} %get-tuple-element.59.r2, ...), custom_call_target="tpu_custom_call" | custom-call | tf_op jit(solution)/shard_map/final/pallas_call | solution.py:356
  (2 shorter events, 0.0 us)
Async XLA Ops:
  0.6 1.2 %copy-start = (f32[32,32,256]{2,1,0:T(8,128)S(1)}, f32[32,32,256]{2,1,0:T(8,128)}, u32[]{:S(2)}) copy-start(f32[32,32,256]{2,1,0:T(8,128)} %r0.1) | copy-start | bytes 3145732
  1.9 1.2 %copy-start.3 = (s32[32,32,256]{2,1,0:T(8,128)S(1)}, s32[32,32,256]{2,1,0:T(8,128)}, u32[]{:S(2)}) copy-start(s32[32,32,256]{2,1,0:T(8,128)} %phase.3) | copy-start | bytes 3145732
  3.1 30.6 %copy-start.2 = (f32[32,32,256]{2,1,0:T(8,128)S(1)}, f32[32,32,256]{2,1,0:T(8,128)}, u32[]{:S(2)}) copy-start(f32[32,32,256]{2,1,0:T(8,128)} %r0.1) | copy-start | bytes 3145732
  3.1 30.6 %copy-start.5 = (f32[4]{0:T(128)S(1)}, f32[4]{0:T(128)}, u32[]{:S(2)}) copy-start(f32[4]{0:T(128)} %table.3) | copy-start | bytes 52
  3.2 16.8 %collective-permute-start = (f32[2,608,128]{2,1,0:T(8,128)S(1)}, f32[2,608,128]{2,1,0:T(8,128)S(1)}, u32[]{:S(2)}, u32[]{:S(2)}) collective-permute-start(f32[2,608,128]{2,1,0:T(8,128)S(1)} %get-tuple-element.34), channel_id=1, source_target_pairs={{0,1},{1,2},{2,3},{3,4},{4,5},{5,6},{6,7},{7,8},{8,9},{9,10},{10,1... | collective-permute-start | bytes 1867784 | tf_op jit(solution)/shard_map/ppermute | solution.py:324
  7.3 16.5 %collective-permute-start.1 = (f32[2,608,128]{2,1,0:T(8,128)S(1)}, f32[2,608,128]{2,1,0:T(8,128)S(1)}, u32[]{:S(2)}, u32[]{:S(2)}) collective-permute-start(f32[2,608,128]{2,1,0:T(8,128)S(1)} %get-tuple-element.35), channel_id=1, source_target_pairs={{1,0},{2,1},{3,2},{4,3},{5,4},{6,5},{7,6},{8,7},{9,8},{10,9},{11,1... | collective-permute-start | bytes 1867784 | tf_op jit(solution)/shard_map/ppermute | solution.py:324
  23.9 1.2 %copy-start.1 = (f32[32,32,256]{2,1,0:T(8,128)S(1)}, f32[32,32,256]{2,1,0:T(8,128)}, u32[]{:S(2)}) copy-start(f32[32,32,256]{2,1,0:T(8,128)} %r0.1) | copy-start | bytes 3145732
  25.1 1.2 %copy-start.4 = (s32[32,32,256]{2,1,0:T(8,128)S(1)}, s32[32,32,256]{2,1,0:T(8,128)}, u32[]{:S(2)}) copy-start(s32[32,32,256]{2,1,0:T(8,128)} %phase.3) | copy-start | bytes 3145732
  26.8 28.2 %collective-permute-start.2 = (f32[19,2,56,128]{3,2,1,0:T(8,128)S(1)}, f32[19,2,56,128]{3,2,1,0:T(8,128)S(1)}, u32[]{:S(2)}, u32[]{:S(2)}) collective-permute-start(f32[19,2,56,128]{3,2,1,0:T(8,128)S(1)} %get-tuple-element.38), channel_id=1, source_target_pairs={{0,16},{16,32},{32,48},{48,64},{64,80},{80,96},{96,112},{1,17},{17... | collective-permute-start | bytes 3268616 | tf_op jit(solution)/shard_map/ppermute | solution.py:324
  31.7 23.3 %collective-permute-start.3 = (f32[19,2,56,128]{3,2,1,0:T(8,128)S(1)}, f32[19,2,56,128]{3,2,1,0:T(8,128)S(1)}, u32[]{:S(2)}, u32[]{:S(2)}) collective-permute-start(f32[19,2,56,128]{3,2,1,0:T(8,128)S(1)} %get-tuple-element.39), channel_id=1, source_target_pairs={{16,0},{32,16},{48,32},{64,48},{80,64},{96,80},{112,96},{17,1},{33... | collective-permute-start | bytes 3268616 | tf_op jit(solution)/shard_map/ppermute | solution.py:324

commit v3 on v2

v3 whole, which is shorter than its diff:
```python
import functools

import jax
import jax.numpy as jnp
from jax import lax
from jax.experimental import pallas as pl
from jax.experimental.pallas import tpu as pltpu
from jax.sharding import PartitionSpec as P

centre_value = 1.1
half_width = 0.9
ratio_sigma = centre_value / half_width
rho_first = 1.0 / ratio_sigma
rho_second = 1.0 / (2.0 * ratio_sigma - rho_first)
rho_third = 1.0 / (2.0 * ratio_sigma - rho_second)
start_scale = 1.0 / centre_value
keep_first = rho_second * rho_first
push_first = 2.0 * rho_second / half_width
keep_second = rho_third * rho_second
push_second = 2.0 * rho_third / half_width

ZT = (1.0 + keep_first - push_first) * start_scale + push_first
ZS = push_first * start_scale
UZ = 1.0 + keep_second - push_second
UT = push_second - keep_second * start_scale
US = push_second

NB = 32
HB = 9
HL = 10
OFF = 12
YE = 56
XE = NB + 2 * HL
NZ = 256
VM = pl.BlockSpec(memory_space=pltpu.VMEM)
SM = pl.BlockSpec(memory_space=pltpu.SMEM)
f32 = jnp.float32


def shape(*dims):
    return jax.ShapeDtypeStruct(dims, f32)


def params(mib):
    return pltpu.CompilerParams(vmem_limit_bytes=mib * 1024 * 1024)

HALF = NZ // 2
FULL, NEAR = (0, YE), (8, YE - 8)
NB_NEAR, NL_NEAR = 4, 5
SENT = (NB_NEAR + NL_NEAR) * YE + (HB - NB_NEAR + HL - NL_NEAR) * (YE - 16)


def rows_of(slab):
    return slice(slab[0], slab[1])


def held(slab):
    return slice(slab[0] + 8, slab[1] + 8)


def sent_rows(distance, label):
    near, far = (NL_NEAR, HL - NL_NEAR) if label else (NB_NEAR, HB - NB_NEAR)
    if distance <= near:
        start = (NB_NEAR * YE if label else 0) + (distance - 1) * YE
        return slice(start, start + YE), FULL
    base = (NB_NEAR + NL_NEAR) * YE + ((HB - NB_NEAR) * (YE - 16) if label else 0)
    start = base + (distance - near - 1) * (YE - 16)
    return slice(start, start + YE - 16), NEAR


def lanes(h):
    return slice(HALF * h, HALF * h + HALF)


def pack_kernel(width, source, up, down, block):
    blank = jnp.zeros((2, 16, HALF), f32)
    for x in range(NB):
        rows = slice(width * x, width * x + width)
        block[x, :, 0:16] = blank
        block[x, :, YE - 16:YE] = blank
        for h in range(2):
            up[h, rows] = source[x, NB - width:NB, lanes(h)].astype(f32)
            down[h, rows] = source[x, 0:width, lanes(h)].astype(f32)
            block[x, h, OFF:OFF + NB] = source[x, :, lanes(h)].astype(f32)


def join_rows(width, low, high, block):
    for x in range(NB):
        rows = slice(width * x, width * x + width)
        for h in range(2):
            block[x, h, OFF - width:OFF] = low[h, rows]
            block[x, h, OFF + NB:OFF + NB + width] = high[h, rows]


def join_label_kernel(low, high, _, block):
    join_rows(HL, low, high, block)


def join_field_kernel(low, high, label, _, __, block, up, down):
    join_rows(HB, low, high, block)
    for source, width in ((block, HB), (label, HL)):
        for d in range(1, width + 1):
            place, slab = sent_rows(d, source is label)
            for h in range(2):
                up[h, place] = source[NB - d, h, rows_of(slab)]
                down[h, place] = source[d - 1, h, rows_of(slab)]


def machine(arrays):
    west, east, south, north, below, above, diag, t, z, u = arrays

    def spread(ref, x, slab, finish):
        lane = lax.broadcasted_iota(jnp.int32, (slab[1] - slab[0], HALF), 1)
        at_low, at_high = lane == 0, lane == HALF - 1
        rows, real = rows_of(slab), held(slab)
        less, more = held((slab[0] - 1, slab[1] - 1)), held((slab[0] + 1, slab[1] + 1))
        here = tuple(ref[x, h, real] for h in range(2))
        back = tuple(pltpu.roll(here[h], 1, 1) for h in range(2))
        ahead = tuple(pltpu.roll(here[h], HALF - 1, 1) for h in range(2))
        lower = (back[0], jnp.where(at_low, back[0], back[1]))
        upper = (jnp.where(at_high, ahead[1], ahead[0]), ahead[1])
        for h in range(2):
            total = (
                (west[x, h, rows] * ref[x - 1, h, real] + east[x, h, rows] * ref[x + 1, h, real])
                + (south[x, h, rows] * ref[x, h, less] + north[x, h, rows] * ref[x, h, more])
                + (below[x, h, rows] * lower[h] + above[x, h, rows] * upper[h])
            )
            finish(h, here[h], total)

    def first(x, slab):
        def finish(h, here, total):
            z[x, h, held(slab)] = ZT * here + ZS * total
        spread(t, x, slab, finish)

    def second(x, slab):
        def finish(h, here, total):
            u[x, h, held(slab)] = UZ * here + UT * t[x, h, held(slab)] + US * total
        spread(z, x, slab, finish)

    def third(x, slab):
        def finish(h, here, total):
            t[x, h, held(slab)] = (t[x, h, held(slab)] - here) + total
        spread(u, x, slab, finish)

    steps = (first, second, third)

    def run(stage, start, stop):
        slab = FULL if stage < 4 else NEAR
        size = stop - start
        chunk = max(k for k in range(1, CHAIN + 1) if size % k == 0)
        if chunk < 5:
            chunk = CHAIN
        middle = stop - size % chunk

        def body(x, _):
            steps[stage % 3](x, slab)
            return 0
        lax.fori_loop(start, middle, body, 0, unroll=chunk)
        for x in range(middle, stop):
            steps[stage % 3](x, slab)

    def run_sides(stage):
        low, high = 2 + stage, HI - 2 - stage
        for slab, lo, hi in (((FULL if stage < 4 else NEAR), low + 5, high),
                             (NEAR, low, high + 5)):
            def body(i, _):
                steps[stage % 3](lo + i, slab)
                steps[stage % 3](hi + i, slab)
                return 0
            lax.fori_loop(0, 5, body, 0, unroll=5)

    def keep(ranges, u_out, r_out, pairs):
        own = slice(8 + OFF, 8 + OFF + NB)
        zero = jnp.zeros((NB, HALF), f32)

        def body(x, carry):
            totals = list(carry)
            for h in range(2):
                pre = u[x, h, own]
                res = t[x, h, own] * diag[x, h, OFF:OFF + NB]
                u_out[x - HL, :, lanes(h)] = pre
                r_out[x - HL, :, lanes(h)] = res
                for k, other in enumerate(pairs):
                    left = res if other is None else other[x - HL, :, lanes(h)]
                    totals[k] = totals[k] + left * pre
            return tuple(totals)

        totals = (zero,) * len(pairs)
        for start, stop in ranges:
            totals = lax.fori_loop(start, stop, body, totals)
        return totals

    return run, run_sides, keep


def kinds(table):
    def kind(labels):
        return jnp.where(labels == 1.0, 0.5 / table[1], jnp.where(
            labels == 2.0, 0.5 / table[2], jnp.where(
                labels == 3.0, 0.5 / table[3], 0.5 / table[0])))
    return kind


def coupler(table, arrays):
    west, east, south, north, below, above, diag, _, z, u = arrays
    lining = 0.5 / table[0]

    def row(x, labels, slab):
        lane = lax.broadcasted_iota(jnp.int32, (slab[1] - slab[0], HALF), 1)
        at_low, at_high = lane == 0, lane == HALF - 1
        rows, real = rows_of(slab), held(slab)
        less, more = held((slab[0] - 1, slab[1] - 1)), held((slab[0] + 1, slab[1] + 1))
        here = tuple(z[x, h, real] for h in range(2))
        after = tuple(pltpu.roll(here[h], HALF - 1, 1) for h in range(2))
        to_up = (1.0 / (here[0] + jnp.where(at_high, after[1], after[0])),
                 1.0 / (here[1] + jnp.where(at_high, lining, after[1])))
        moved = tuple(pltpu.roll(to_up[h], 1, 1) for h in range(2))
        to_down = (jnp.where(at_low, 1.0 / (here[0] + lining), moved[0]),
                   jnp.where(at_low, moved[0], moved[1]))
        for h in range(2):
            to_west = 1.0 / (here[h] + z[x - 1, h, real])
            to_east = 1.0 / (here[h] + z[x + 1, h, real])
            to_south = 1.0 / (here[h] + z[x, h, less])
            to_north = 1.0 / (here[h] + z[x, h, more])
            whole = to_west + to_east + to_south + to_north + to_down[h] + to_up[h]
            inverse = jnp.where(labels[h] > 0.0, 1.0 / whole, 0.0)
            west[x, h, rows] = to_west * inverse
            east[x, h, rows] = to_east * inverse
            south[x, h, rows] = to_south * inverse
            north[x, h, rows] = to_north * inverse
            down = to_down[h] * inverse
            rise = to_up[h] * inverse
            below[x, h, rows] = jnp.where(at_low, 0.0, down) if h == 0 else down
            above[x, h, rows] = jnp.where(at_high, 0.0, rise) if h == 1 else rise
            u[x, h, real] = inverse
            diag[x, h, rows] = whole

    return row


def as_line(parts):
    place = lax.broadcasted_iota(jnp.int32, (8, 128), 1)
    line = jnp.zeros((8, 128), f32)
    for k, part in enumerate(parts):
        line = jnp.where(place == k, jnp.sum(part), line)
    return line


LO, HI = HL, HL + NB
ROWS = 2 * HL


def own_kernel(table, label, *arrays):
    t, z, u = arrays[7:]
    kind = kinds(table)

    def clear(x, _):
        for ref in (t, z, u):
            ref[x, :, 0:8] = jnp.zeros((2, 8, HALF), f32)
            ref[x, :, 8 + YE:16 + YE] = jnp.zeros((2, 8, HALF), f32)
        return 0

    def clear_side(x, _):
        for side in (x, HI + x):
            for ref in (t, z, u):
                ref[side, :, 0:16] = jnp.zeros((2, 16, HALF), f32)
                ref[side, :, YE:16 + YE] = jnp.zeros((2, 16, HALF), f32)
        return 0
    lax.fori_loop(LO, HI, clear, 0, unroll=4)
    lax.fori_loop(0, HL, clear_side, 0, unroll=2)

    def translate(x, _):
        z[x + HL, :, 8:8 + YE] = kind(label[x])
        return 0
    lax.fori_loop(0, NB, translate, 0, unroll=2)
    row = coupler(table, arrays)

    def body(x, _):
        row(x, label[x - HL], FULL)
        return 0
    lax.fori_loop(LO + 1, HI - 1, body, 0, unroll=CU)


CU = 3
CHAIN = 8


def inner_kernel(rhs, field, *refs):
    arrays = refs[0:7] + refs[10:13]
    (r1, r2, r3, u0, u1, u2), sums = refs[13:19], refs[19]
    t, z, u = arrays[7:]
    run, _, keep = machine(arrays)

    def begin(x, _):
        t[x, :, 8:8 + YE] = field[x - HL] * u[x, :, 8:8 + YE]
        return 0
    lax.fori_loop(LO + 1, HI - 1, begin, 0, unroll=2)
    parts = ()
    for stage in range(9):
        rows = (LO + 2 + stage, HI - 2 - stage)
        run(stage, *rows)
        if stage == 2:
            parts += keep((rows,), u0, r1, (rhs, None))
        if stage == 5:
            parts += keep((rows,), u1, r2, (r1, None))
        if stage == 8:
            keep((rows,), u2, r3, ())
    sums[...] = as_line(parts)


def outer_kernel(table, rhs, label, field, low, high, part_sums, *refs):
    arrays = refs[16:26]
    (r1, r2, r3, u0, u1, u2), sums = refs[26:32], refs[32]
    t, z, u = arrays[7:]
    kind = kinds(table)
    row = coupler(table, arrays)
    for d in range(1, HL + 1):
        place, slab = sent_rows(d, True)
        for h in range(2):
            z[LO - d, h, held(slab)] = kind(low[h, place])
            z[HI - 1 + d, h, held(slab)] = kind(high[h, place])
    for x, k in ((LO, 0), (HI - 1, NB - 1)):
        row(x, label[k], FULL)
        t[x, :, held(FULL)] = field[k] * u[x, :, held(FULL)]

    def couple(d, slab, place, value):
        for x, source in ((LO - d, low), (HI - 1 + d, high)):
            row(x, tuple(source[h, place] for h in range(2)), slab)
            for h in range(2):
                t[x, h, held(slab)] = source[h, value] * u[x, h, held(slab)]

    for d in range(1, HB + 1):
        value, slab = sent_rows(d, False)
        place, whole = sent_rows(d, True)
        if whole != slab:
            place = slice(place.start + 8, place.stop - 8)
        couple(d, slab, place, value)
    _, run_sides, keep = machine(arrays)
    parts = ()
    for stage in range(9):
        run_sides(stage)
        rest = ((LO, LO + 2 + stage), (HI - 2 - stage, HI))
        if stage == 2:
            parts += keep(rest, u0, r1, (rhs, None))
        if stage == 5:
            parts += keep(rest, u1, r2, (r1, None))
        if stage == 8:
            keep(rest, u2, r3, ())
    sums[...] = part_sums[...] + as_line(parts)


CHUNK = 4


def final_kernel(sums, r0, r1, r2, r3, u0, u1, u2, solution_out, residual_out, pre_out,
                 image_out, bufs, sems):
    lane = lax.broadcasted_iota(jnp.int32, (8, 128), 1)
    total = sums[0:8, :]
    for k in range(1, 16):
        total = total + sums[8 * k:8 * k + 8, :]
    m0, m1, m2, m3 = (jnp.sum(jnp.where(lane == k, total, 0.0), axis=(0, 1), keepdims=True)
                      for k in range(4))
    curvature = m0 - m1
    step_one = m0 / curvature
    off_one = -m1 / curvature
    energy = off_one * off_one * m0 + 2.0 * off_one * step_one * m1 + step_one * step_one * m2
    bend = (off_one * off_one * (m0 - m1) + 2.0 * off_one * step_one * (m1 - m2)
            + step_one * step_one * (m2 - m3))
    momentum = energy / m0
    step_two = energy / (bend - momentum * energy / step_one)
    c2 = step_one * step_two
    c1 = step_one + step_two * (1.0 + momentum) - 2.0 * c2
    c0 = off_one * (1.0 - step_two) - step_two * momentum
    s0 = c1 + c2
    outs = (solution_out, residual_out, pre_out, image_out)
    copies = []
    for chunk in range(NB // CHUNK):
        def body(k, _):
            x = chunk * CHUNK + k
            v0, v1, v2, v3 = r0[x], r1[x], r2[x], r3[x]
            w0, w1, w2 = u0[x], u1[x], u2[x]
            bufs[0, x] = s0 * w0 + c2 * w1
            bufs[1, x] = c0 * v0 + c1 * v1 + c2 * v2
            bufs[2, x] = c0 * w0 + c1 * w1 + c2 * w2
            bufs[3, x] = c0 * (v0 - v1) + c1 * (v1 - v2) + c2 * (v2 - v3)
            return 0
        lax.fori_loop(0, CHUNK, body, 0)
        rows = slice(chunk * CHUNK, (chunk + 1) * CHUNK)
        for k in range(4):
            copy = pltpu.make_async_copy(bufs.at[k, rows], outs[k].at[rows], sems.at[chunk, k])
            copy.start()
            copies.append(copy)
    for copy in copies:
        copy.wait()


def neighbours(axis):
    count = lax.axis_size(axis)
    forward = [(i, i + 1) for i in range(count - 1)]
    return forward, [(target, source) for source, target in forward]


def swap(up, down, axis):
    forward, backward = neighbours(axis)
    return lax.ppermute(up, axis, forward), lax.ppermute(down, axis, backward)


def local(right_side, phase, table):
    def call(kernel, name, outs, ins, args, mib=2, cost=1, alias=(), scratch=()):
        return pl.pallas_call(
            kernel, name=name, in_specs=ins, out_specs=[VM] * len(outs), out_shape=outs,
            scratch_shapes=list(scratch), compiler_params=params(mib),
            input_output_aliases=dict(alias),
            cost_estimate=pl.CostEstimate(
                flops=0, bytes_accessed=int(cost * 2.5e6), transcendentals=0),
        )(*args)

    brick = shape(NB, NB, NZ)
    block = shape(NB, 2, YE, HALF)
    line = shape(8, 128)
    state = [shape(XE, 2, YE, HALF)] * 7 + [shape(XE, 2, YE + 16, HALF)] * 3

    def pack(source, width, name):
        return call(functools.partial(pack_kernel, width), name,
                    [shape(2, NB * width, HALF)] * 2 + [block], [VM], (source,))

    up_l, down_l, label = pack(phase, HL, "packlabel")
    up_f, down_f, field = pack(right_side, HB, "packfield")
    low_l, high_l = swap(up_l, down_l, "gy")
    low_f, high_f = swap(up_f, down_f, "gy")
    (label,) = call(join_label_kernel, "joinlabel", [block], [VM] * 3,
                    (low_l, high_l, label), alias={2: 0})
    arrays = call(own_kernel, "own", state, [SM, VM], (table, label), cost=5)
    field, up, down = call(
        join_field_kernel, "joinfield", [block] + [shape(2, SENT, HALF)] * 2,
        [VM] * 5, (low_f, high_f, label, arrays[9], field), alias={4: 0})
    low, high = swap(up, down, "gx")
    *mats, t, z, u = arrays
    *refs, sums = call(
        inner_kernel, "inner", state[7:] + [brick] * 6 + [line], [VM] * 12,
        (right_side, field, *mats, t, z, u), cost=10, alias={9 + k: k for k in range(3)})
    *refs, sums = call(
        outer_kernel, "outer", state + [brick] * 6 + [line], [SM] + [VM] * 22,
        (table, right_side, label, field, low, high, sums, *mats, *refs),
        cost=20, alias={7 + k: k for k in range(16)})
    r1, r2, r3, u0, u1, u2 = refs[10:]
    gathered = lax.all_to_all(
        jnp.broadcast_to(sums[0:1], (128, 128)), ("gx", "gy"), 0, 0, tiled=True)
    hbm = pl.BlockSpec(memory_space=pl.ANY)
    return pl.pallas_call(
        final_kernel, name="final", in_specs=[VM] * 8, out_specs=[hbm] * 4,
        out_shape=[brick] * 4,
        scratch_shapes=[pltpu.VMEM((4, NB, NB, NZ), f32),
                        pltpu.SemaphoreType.DMA((NB // CHUNK, 4))],
        compiler_params=params(6),
    )(gathered, right_side, r1, r2, r3, u0, u1, u2)


def solution(mesh):
    placed = (P("gx", "gy", None), P("gx", "gy", None), P())
    return jax.shard_map(
        local,
        mesh=mesh,
        in_specs=placed,
        out_specs=(P("gx", "gy", None),) * 4,
        check_vma=False,
    )
```

time: 101 us -> 79.4 us (0.79)
  Pallas kernels: 45.2 us -> 30.8 us
  waiting for transfers between devices: 15.2 us -> 4.36 us
  starting transfers between devices: 12.2 us -> 17.6 us
  local copies, waits for them, and re-layouts: 4.94 us -> 2.48 us
  blocking collectives: 21.9 us -> 23 us
    pallas_call x4 -> x7, Pallas kernels: 40.1 us -> 28.3 us  [call(): pl.pallas_call(kernel, name=name, in_specs=ins, out_specs=[VM] * len(outs...]
    ppermute x4 -> x6, waiting for transfers between devices: 15.2 us -> 4.36 us  [swap(): return (lax.ppermute(up, axis, forward), lax.ppermute(down, axis, backward))]
    ppermute x4 -> x6, starting transfers between devices: 12.2 us -> 17.6 us  [swap(): return (lax.ppermute(up, axis, forward), lax.ppermute(down, axis, backward))]
    pallas_call x1, Pallas kernels: 5.1 us -> 2.53 us  [local(): pl.pallas_call(final_kernel, name='final', in_specs=[VM] * 8, out_specs=[...]
    unnamed x12 -> x8, local copies, waits for them, and re-layouts: 4.9 us -> 2.45 us
    all_to_all x1, blocking collectives: 21.9 us -> 23 us  [local(): lax.all_to_all(jnp.broadcast_to(sums[0:1], (128, 128)), ('gx', 'gy'), 0,...]
  transfers between devices with their start and end apart: 4 -> 6, of which waited for: 2 -> 3; matrix products, arithmetic and copies ran while one was open for 0% -> 0% of each run, Pallas kernels for 21% -> 21%
where the time goes in v3:
time: 79.4 us; the launch traced here: 79 us
  Pallas kernels  30.8 us (39%)
  blocking collectives  23 us (29%)
  starting transfers between devices  17.6 us (22%)
  waiting for transfers between devices  4.36 us (5%)
  local copies, waits for them, and re-layouts  2.48 us (3%)
    pallas_call x7, Pallas kernels, call(): pl.pallas_call(kernel, name=name, in_specs=ins, out_specs=[VM] * len(outs...  28.3 us
    all_to_all x1, blocking collectives, local(): lax.all_to_all(jnp.broadcast_to(sums[0:1], (128, 128)), ('gx', 'gy'), 0,...  23 us
    ppermute x6, starting transfers between devices, swap(): return (lax.ppermute(up, axis, forward), lax.ppermute(down, axis, backward))  17.6 us
    ppermute x6, waiting for transfers between devices, swap(): return (lax.ppermute(up, axis, forward), lax.ppermute(down, axis, backward))  4.36 us
    pallas_call x1, Pallas kernels, local(): pl.pallas_call(final_kernel, name='final', in_specs=[VM] * 8, out_specs=[...  2.53 us
    unnamed x8, local copies, waits for them, and re-layouts  2.45 us
  transfers between devices with their start and end apart: 6, of which 3 were waited for; matrix products, arithmetic and copies ran while one was open for 0% of the time, Pallas kernels for 21%

profile of v3, /device:TPU:1, one launch (start us, length us, event | category | flops | bytes accessed | tf_op | source)
XLA Modules:
  0.0 79.0 jit_solution(2456816147430285630)
XLA Ops:
  0.6 0.0 copy-start.2
  0.6 1.2 %copy-done.2 = s32[32,32,256]{2,1,0:T(8,128)S(1)} copy-done((s32[32,32,256]{2,1,0:T(8,128)S(1)}, s32[32,32,256]{2,1,0:T(8,128)}, u32[]{:S(2)}) %copy-start.2) | copy-done | bytes 1048600
  1.9 0.0 copy-start.3
  1.9 0.2 packlabel.1
  2.1 4.0 %collective-permute-start = (f32[2,320,128]{2,1,0:T(8,128)S(1)}, f32[2,320,128]{2,1,0:T(8,128)S(1)}, u32[]{:S(2)}, u32[]{:S(2)}) collective-permute-start(f32[2,320,128]{2,1,0:T(8,128)S(1)} %get-tuple-element.40), channel_id=1, source_target_pairs={{0,1},{1,2},{2,3},{3,4},{4,5},{5,6},{6,7},{7,8},{8,9},{9,10},{10,1... | collective-permute-start | bytes 983048 | tf_op jit(solution)/shard_map/ppermute | solution.py:405
  6.0 1.3 %collective-permute-start.1 = (f32[2,320,128]{2,1,0:T(8,128)S(1)}, f32[2,320,128]{2,1,0:T(8,128)S(1)}, u32[]{:S(2)}, u32[]{:S(2)}) collective-permute-start(f32[2,320,128]{2,1,0:T(8,128)S(1)} %get-tuple-element.41), channel_id=1, source_target_pairs={{1,0},{2,1},{3,2},{4,3},{5,4},{6,5},{7,6},{8,7},{9,8},{10,9},{11,1... | collective-permute-start | bytes 983048 | tf_op jit(solution)/shard_map/ppermute | solution.py:405
  7.3 0.0 copy-start
  7.3 1.2 %copy-done = f32[32,32,256]{2,1,0:T(8,128)S(1)} copy-done((f32[32,32,256]{2,1,0:T(8,128)S(1)}, f32[32,32,256]{2,1,0:T(8,128)}, u32[]{:S(2)}) %copy-start) | copy-done | bytes 1048600
  8.6 0.2 packfield.1
  8.8 4.0 %collective-permute-start.2 = (f32[2,288,128]{2,1,0:T(8,128)S(1)}, f32[2,288,128]{2,1,0:T(8,128)S(1)}, u32[]{:S(2)}, u32[]{:S(2)}) collective-permute-start(f32[2,288,128]{2,1,0:T(8,128)S(1)} %get-tuple-element.43), channel_id=1, source_target_pairs={{0,1},{1,2},{2,3},{3,4},{4,5},{5,6},{6,7},{7,8},{8,9},{9,10},{10,1... | collective-permute-start | bytes 884744 | tf_op jit(solution)/shard_map/ppermute | solution.py:405
  12.8 1.3 %collective-permute-start.3 = (f32[2,288,128]{2,1,0:T(8,128)S(1)}, f32[2,288,128]{2,1,0:T(8,128)S(1)}, u32[]{:S(2)}, u32[]{:S(2)}) collective-permute-start(f32[2,288,128]{2,1,0:T(8,128)S(1)} %get-tuple-element.44), channel_id=1, source_target_pairs={{1,0},{2,1},{3,2},{4,3},{5,4},{6,5},{7,6},{8,7},{9,8},{10,9},{11,1... | collective-permute-start | bytes 884744 | tf_op jit(solution)/shard_map/ppermute | solution.py:405
  14.1 0.0 collective-permute-done.low
  14.1 2.2 %collective-permute-done.1.high = f32[2,320,128]{2,1,0:T(8,128)S(1)} collective-permute-done((f32[2,320,128]{2,1,0:T(8,128)S(1)}, f32[2,320,128]{2,1,0:T(8,128)S(1)}, u32[]{:S(2)}, u32[]{:S(2)}) %collective-permute-start.1) | collective-permute-done | bytes 327712 | tf_op jit(solution)/shard_map/ppermute | solution.py:405
  16.2 0.1 joinlabel.1.label
  16.3 0.0 copy-done.3
  16.3 4.7 %own.1 = (f32[52,2,56,128]{3,2,1,0:T(8,128)S(1)}, f32[52,2,56,128]{3,2,1,0:T(8,128)S(1)}, f32[52,2,56,128]{3,2,1,0:T(8,128)S(1)}, f32[52,2,56,128]{3,2,1,0:T(8,1...) custom-call(f32[4]{0:T(128)S(1)} %copy-done.3, ...), custom_call_target="tpu_custom_call" | custom-call | bytes 12500000 | tf_op jit(solution)/shard_map/own/pallas_call | solution.py:410
  21.0 0.0 collective-permute-done.2.low
  21.0 1.2 %collective-permute-done.3.high = f32[2,288,128]{2,1,0:T(8,128)S(1)} collective-permute-done((f32[2,288,128]{2,1,0:T(8,128)S(1)}, f32[2,288,128]{2,1,0:T(8,128)S(1)}, u32[]{:S(2)}, u32[]{:S(2)}) %collective-permute-start.3) | collective-permute-done | bytes 294944 | tf_op jit(solution)/shard_map/ppermute | solution.py:405
  22.3 0.2 joinfield.1
  22.5 5.2 %collective-permute-start.4 = (f32[2,904,128]{2,1,0:T(8,128)S(1)}, f32[2,904,128]{2,1,0:T(8,128)S(1)}, u32[]{:S(2)}, u32[]{:S(2)}) collective-permute-start(f32[2,904,128]{2,1,0:T(8,128)S(1)} %get-tuple-element.48), channel_id=1, source_target_pairs={{0,16},{16,32},{32,48},{48,64},{64,80},{80,96},{96,112},{1,17},{17... | collective-permute-start | bytes 2777096 | tf_op jit(solution)/shard_map/ppermute | solution.py:405
  27.7 1.9 %collective-permute-start.5 = (f32[2,904,128]{2,1,0:T(8,128)S(1)}, f32[2,904,128]{2,1,0:T(8,128)S(1)}, u32[]{:S(2)}, u32[]{:S(2)}) collective-permute-start(f32[2,904,128]{2,1,0:T(8,128)S(1)} %get-tuple-element.49), channel_id=1, source_target_pairs={{16,0},{32,16},{48,32},{64,48},{80,64},{96,80},{112,96},{17,1},{33... | collective-permute-start | bytes 2777096 | tf_op jit(solution)/shard_map/ppermute | solution.py:405
  29.6 11.9 %inner.1 = (f32[52,2,72,128]{3,2,1,0:T(8,128)S(1)}, f32[52,2,72,128]{3,2,1,0:T(8,128)S(1)}, f32[52,2,72,128]{3,2,1,0:T(8,128)S(1)}, f32[32,32,256]{2,1,0:T(8,128...) custom-call(f32[32,32,256]{2,1,0:T(8,128)S(1)} %copy-done, ...), custom_call_target="tpu_custom_call", output_to_operand_aliasing={{0}: (9, {}), {1}: (10, {}), {2}: (11, {})} | custom-call | bytes 25000000 | tf_op jit(solution)/shard_map/inner/pallas_call | solution.py:410
  41.5 0.0 collective-permute-done.4.low
  41.5 1.0 %collective-permute-done.5.high = f32[2,904,128]{2,1,0:T(8,128)S(1)} collective-permute-done((f32[2,904,128]{2,1,0:T(8,128)S(1)}, f32[2,904,128]{2,1,0:T(8,128)S(1)}, u32[]{:S(2)}, u32[]{:S(2)}) %collective-permute-start.5) | collective-permute-done | bytes 925728 | tf_op jit(solution)/shard_map/ppermute | solution.py:405
  42.5 0.0 copy-start.1
  42.5 11.0 %outer.1 = (f32[52,2,56,128]{3,2,1,0:T(8,128)S(1)}, f32[52,2,56,128]{3,2,1,0:T(8,128)S(1)}, f32[52,2,56,128]{3,2,1,0:T(8,128)S(1)}, f32[52,2,56,128]{3,2,1,0:T(8...) custom-call(f32[4]{0:T(128)S(1)} %copy-done.3, ...), custom_call_target="tpu_custom_call", output_to_operand_aliasing={{0}: (7, {}), {1}: (8, {}), {2}: (9, {}), {3}: (10, {}), {4... | custom-call | bytes 50000000 | tf_op jit(solution)/shard_map/outer/pallas_call | solution.py:410
  53.5 23.0 %all_to_all.8 = f32[128,1,128]{2,1,0:T(1,128)S(1)} all-to-all(f32[128,1,128]{2,1,0:T(1,128)S(1)} %broadcast_in_dim.2), channel_id=1, replica_groups=mesh['gx'=8,'gy'=16] {'gx','gy'}, dimensions={0} | all-to-all | bytes 131072 | tf_op jit(solution)/shard_map/all_to_all | solution.py:447
  76.5 0.0 copy-done.1
  76.5 2.5 %final.1 = (f32[32,32,256]{2,1,0:T(8,128)}, f32[32,32,256]{2,1,0:T(8,128)}, f32[32,32,256]{2,1,0:T(8,128)}, f32[32,32,256]{2,1,0:T(8,128)}) custom-call(f32[128,128]{1,0:T(8,128)S(1)} %bitcast.3, f32[32,32,256]{2,1,0:T(8,128)S(1)} %copy-done.1, f32[32,32,256]{2,1,0:T(8,128)S(1)} %get-tuple-element.70.r1, f32[32,32,256]{2,1,0:T(8,128)S(1)} %get-tuple-element.71.r2, ...), custom_call_target="tpu_custom_call" | custom-call | tf_op jit(solution)/shard_map/final/pallas_call | solution.py:450
  (2 shorter events, 0.0 us)
Async XLA Ops:
  0.6 1.2 %copy-start.2 = (s32[32,32,256]{2,1,0:T(8,128)S(1)}, s32[32,32,256]{2,1,0:T(8,128)}, u32[]{:S(2)}) copy-start(s32[32,32,256]{2,1,0:T(8,128)} %source.2) | copy-start | bytes 3145732
  1.9 14.5 %copy-start.3 = (f32[4]{0:T(128)S(1)}, f32[4]{0:T(128)}, u32[]{:S(2)}) copy-start(f32[4]{0:T(128)} %table.3) | copy-start | bytes 52
  2.1 12.0 %collective-permute-start = (f32[2,320,128]{2,1,0:T(8,128)S(1)}, f32[2,320,128]{2,1,0:T(8,128)S(1)}, u32[]{:S(2)}, u32[]{:S(2)}) collective-permute-start(f32[2,320,128]{2,1,0:T(8,128)S(1)} %get-tuple-element.40), channel_id=1, source_target_pairs={{0,1},{1,2},{2,3},{3,4},{4,5},{5,6},{6,7},{7,8},{8,9},{9,10},{10,1... | collective-permute-start | bytes 983048 | tf_op jit(solution)/shard_map/ppermute | solution.py:405
  6.0 10.2 %collective-permute-start.1 = (f32[2,320,128]{2,1,0:T(8,128)S(1)}, f32[2,320,128]{2,1,0:T(8,128)S(1)}, u32[]{:S(2)}, u32[]{:S(2)}) collective-permute-start(f32[2,320,128]{2,1,0:T(8,128)S(1)} %get-tuple-element.41), channel_id=1, source_target_pairs={{1,0},{2,1},{3,2},{4,3},{5,4},{6,5},{7,6},{8,7},{9,8},{10,9},{11,1... | collective-permute-start | bytes 983048 | tf_op jit(solution)/shard_map/ppermute | solution.py:405
  7.3 1.2 %copy-start = (f32[32,32,256]{2,1,0:T(8,128)S(1)}, f32[32,32,256]{2,1,0:T(8,128)}, u32[]{:S(2)}) copy-start(f32[32,32,256]{2,1,0:T(8,128)} %r0.1) | copy-start | bytes 3145732
  8.8 12.3 %collective-permute-start.2 = (f32[2,288,128]{2,1,0:T(8,128)S(1)}, f32[2,288,128]{2,1,0:T(8,128)S(1)}, u32[]{:S(2)}, u32[]{:S(2)}) collective-permute-start(f32[2,288,128]{2,1,0:T(8,128)S(1)} %get-tuple-element.43), channel_id=1, source_target_pairs={{0,1},{1,2},{2,3},{3,4},{4,5},{5,6},{6,7},{7,8},{8,9},{9,10},{10,1... | collective-permute-start | bytes 884744 | tf_op jit(solution)/shard_map/ppermute | solution.py:405
  12.8 9.5 %collective-permute-start.3 = (f32[2,288,128]{2,1,0:T(8,128)S(1)}, f32[2,288,128]{2,1,0:T(8,128)S(1)}, u32[]{:S(2)}, u32[]{:S(2)}) collective-permute-start(f32[2,288,128]{2,1,0:T(8,128)S(1)} %get-tuple-element.44), channel_id=1, source_target_pairs={{1,0},{2,1},{3,2},{4,3},{5,4},{6,5},{7,6},{8,7},{9,8},{10,9},{11,1... | collective-permute-start | bytes 884744 | tf_op jit(solution)/shard_map/ppermute | solution.py:405
  22.5 19.0 %collective-permute-start.4 = (f32[2,904,128]{2,1,0:T(8,128)S(1)}, f32[2,904,128]{2,1,0:T(8,128)S(1)}, u32[]{:S(2)}, u32[]{:S(2)}) collective-permute-start(f32[2,904,128]{2,1,0:T(8,128)S(1)} %get-tuple-element.48), channel_id=1, source_target_pairs={{0,16},{16,32},{32,48},{48,64},{64,80},{80,96},{96,112},{1,17},{17... | collective-permute-start | bytes 2777096 | tf_op jit(solution)/shard_map/ppermute | solution.py:405
  27.7 14.8 %collective-permute-start.5 = (f32[2,904,128]{2,1,0:T(8,128)S(1)}, f32[2,904,128]{2,1,0:T(8,128)S(1)}, u32[]{:S(2)}, u32[]{:S(2)}) collective-permute-start(f32[2,904,128]{2,1,0:T(8,128)S(1)} %get-tuple-element.49), channel_id=1, source_target_pairs={{16,0},{32,16},{48,32},{64,48},{80,64},{96,80},{112,96},{17,1},{33... | collective-permute-start | bytes 2777096 | tf_op jit(solution)/shard_map/ppermute | solution.py:405
  42.5 34.0 %copy-start.1 = (f32[32,32,256]{2,1,0:T(8,128)S(1)}, f32[32,32,256]{2,1,0:T(8,128)}, u32[]{:S(2)}) copy-start(f32[32,32,256]{2,1,0:T(8,128)} %r0.1) | copy-start | bytes 3145732

commit v4 on v3

--- a/solution.py
+++ b/solution.py
@@ -46,8 +46,6 @@
 
 HALF = NZ // 2
 FULL, NEAR = (0, YE), (8, YE - 8)
-NB_NEAR, NL_NEAR = 4, 5
-SENT = (NB_NEAR + NL_NEAR) * YE + (HB - NB_NEAR + HL - NL_NEAR) * (YE - 16)
 
 
 def rows_of(slab):
@@ -58,52 +56,76 @@
     return slice(slab[0] + 8, slab[1] + 8)
 
 
-def sent_rows(distance, label):
-    near, far = (NL_NEAR, HL - NL_NEAR) if label else (NB_NEAR, HB - NB_NEAR)
-    if distance <= near:
-        start = (NB_NEAR * YE if label else 0) + (distance - 1) * YE
-        return slice(start, start + YE), FULL
-    base = (NB_NEAR + NL_NEAR) * YE + ((HB - NB_NEAR) * (YE - 16) if label else 0)
-    start = base + (distance - near - 1) * (YE - 16)
-    return slice(start, start + YE - 16), NEAR
+def sent_rows(distance, width):
+    def size(d):
+        return NB + 2 * (width - d)
+    start = sum(size(d) for d in range(1, distance))
+    if width == HL:
+        start += sum(NB + 2 * (HB - d) for d in range(1, HB + 1))
+    off = width - distance
+    return slice(start, start + size(distance)), (OFF - off, OFF + NB + off)
+
+
+SENT = -(-sent_rows(HL, HL)[0].stop // 8) * 8
 
 
 def lanes(h):
     return slice(HALF * h, HALF * h + HALF)
 
 
-def pack_kernel(width, source, up, down, block):
+def by_parity(axis, body, pair, other):
+    odd = lax.rem(lax.axis_index(axis), 2)
+
+    @pl.when(odd == 0)
+    def _():
+        body(pair, other)
+
+    @pl.when(odd == 1)
+    def _():
+        body(other, pair)
+
+
+def pack_kernel(width, source, pair, other, block):
+    def send(up, down):
+        for x in range(NB):
+            rows = slice(width * x, width * x + width)
+            for h in range(2):
+                up[h, rows] = source[x, NB - width:NB, lanes(h)].astype(f32)
+                down[h, rows] = source[x, 0:width, lanes(h)].astype(f32)
+    by_parity("gy", send, pair, other)
     blank = jnp.zeros((2, 16, HALF), f32)
     for x in range(NB):
-        rows = slice(width * x, width * x + width)
         block[x, :, 0:16] = blank
         block[x, :, YE - 16:YE] = blank
         for h in range(2):
-            up[h, rows] = source[x, NB - width:NB, lanes(h)].astype(f32)
-            down[h, rows] = source[x, 0:width, lanes(h)].astype(f32)
             block[x, h, OFF:OFF + NB] = source[x, :, lanes(h)].astype(f32)
 
 
-def join_rows(width, low, high, block):
-    for x in range(NB):
-        rows = slice(width * x, width * x + width)
-        for h in range(2):
-            block[x, h, OFF - width:OFF] = low[h, rows]
-            block[x, h, OFF + NB:OFF + NB + width] = high[h, rows]
-
-
-def join_label_kernel(low, high, _, block):
-    join_rows(HL, low, high, block)
-
-
-def join_field_kernel(low, high, label, _, __, block, up, down):
-    join_rows(HB, low, high, block)
-    for source, width in ((block, HB), (label, HL)):
-        for d in range(1, width + 1):
-            place, slab = sent_rows(d, source is label)
+def join_rows(width, pair, other, block):
+    def take(high, low):
+        for x in range(NB):
+            rows = slice(width * x, width * x + width)
             for h in range(2):
-                up[h, place] = source[NB - d, h, rows_of(slab)]
-                down[h, place] = source[d - 1, h, rows_of(slab)]
+                block[x, h, OFF - width:OFF] = low[h, rows]
+                block[x, h, OFF + NB:OFF + NB + width] = high[h, rows]
+    by_parity("gy", take, pair, other)
+
+
+def join_label_kernel(pair, other, _, block):
+    join_rows(HL, pair, other, block)
+
+
+def join_field_kernel(pair, other, label, _, __, block, pair_x, other_x):
+    join_rows(HB, pair, other, block)
+
+    def send(up, down):
+        for source, width in ((block, HB), (label, HL)):
+            for d in range(1, width + 1):
+                place, slab = sent_rows(d, width)
+                for h in range(2):
+                    up[h, place] = source[NB - d, h, rows_of(slab)]
+                    down[h, place] = source[d - 1, h, rows_of(slab)]
+    by_parity("gx", send, pair_x, other_x)
 
 
 def machine(arrays):
@@ -205,7 +227,7 @@
     west, east, south, north, below, above, diag, _, z, u = arrays
     lining = 0.5 / table[0]
 
-    def row(x, labels, slab):
+    def row(x, marks, slab):
         lane = lax.broadcasted_iota(jnp.int32, (slab[1] - slab[0], HALF), 1)
         at_low, at_high = lane == 0, lane == HALF - 1
         rows, real = rows_of(slab), held(slab)
@@ -223,7 +245,7 @@
             to_south = 1.0 / (here[h] + z[x, h, less])
             to_north = 1.0 / (here[h] + z[x, h, more])
             whole = to_west + to_east + to_south + to_north + to_down[h] + to_up[h]
-            inverse = jnp.where(labels[h] > 0.0, 1.0 / whole, 0.0)
+            inverse = jnp.where(marks[h] > 0.0, 1.0 / whole, 0.0)
             west[x, h, rows] = to_west * inverse
             east[x, h, rows] = to_east * inverse
             south[x, h, rows] = to_south * inverse
@@ -262,9 +284,9 @@
 
     def clear_side(x, _):
         for side in (x, HI + x):
-            for ref in (t, z, u):
-                ref[side, :, 0:16] = jnp.zeros((2, 16, HALF), f32)
-                ref[side, :, YE:16 + YE] = jnp.zeros((2, 16, HALF), f32)
+            t[side] = jnp.zeros((2, YE + 16, HALF), f32)
+            z[side] = jnp.ones((2, YE + 16, HALF), f32)
+            u[side] = jnp.zeros((2, YE + 16, HALF), f32)
         return 0
     lax.fori_loop(LO, HI, clear, 0, unroll=4)
     lax.fori_loop(0, HL, clear_side, 0, unroll=2)
@@ -282,7 +304,7 @@
 
 
 CU = 3
-CHAIN = 8
+CHAIN = 14
 
 
 def inner_kernel(rhs, field, *refs):
@@ -308,33 +330,33 @@
     sums[...] = as_line(parts)
 
 
-def outer_kernel(table, rhs, label, field, low, high, part_sums, *refs):
+def outer_kernel(table, rhs, label, field, pair, other, part_sums, *refs):
     arrays = refs[16:26]
     (r1, r2, r3, u0, u1, u2), sums = refs[26:32], refs[32]
     t, z, u = arrays[7:]
     kind = kinds(table)
     row = coupler(table, arrays)
-    for d in range(1, HL + 1):
-        place, slab = sent_rows(d, True)
-        for h in range(2):
-            z[LO - d, h, held(slab)] = kind(low[h, place])
-            z[HI - 1 + d, h, held(slab)] = kind(high[h, place])
+    def take(high, low):
+        for d in range(1, HL + 1):
+            place, cells = sent_rows(d, HL)
+            for x, source in ((LO - d, low), (HI - 1 + d, high)):
+                for h in range(2):
+                    z[x, h, held(cells)] = kind(source[h, place])
+                    u[x, h, held(cells)] = source[h, place]
+        for d in range(1, HB + 1):
+            place, cells = sent_rows(d, HB)
+            for x, source in ((LO - d, low), (HI - 1 + d, high)):
+                for h in range(2):
+                    t[x, h, held(cells)] = source[h, place]
+    by_parity("gx", take, pair, other)
     for x, k in ((LO, 0), (HI - 1, NB - 1)):
         row(x, label[k], FULL)
         t[x, :, held(FULL)] = field[k] * u[x, :, held(FULL)]
-
-    def couple(d, slab, place, value):
-        for x, source in ((LO - d, low), (HI - 1 + d, high)):
-            row(x, tuple(source[h, place] for h in range(2)), slab)
-            for h in range(2):
-                t[x, h, held(slab)] = source[h, value] * u[x, h, held(slab)]
-
     for d in range(1, HB + 1):
-        value, slab = sent_rows(d, False)
-        place, whole = sent_rows(d, True)
-        if whole != slab:
-            place = slice(place.start + 8, place.stop - 8)
-        couple(d, slab, place, value)
+        slab = FULL if d < 5 else NEAR
+        for x in (LO - d, HI - 1 + d):
+            row(x, tuple(u[x, h, held(slab)] for h in range(2)), slab)
+            t[x, :, held(slab)] = t[x, :, held(slab)] * u[x, :, held(slab)]
     _, run_sides, keep = machine(arrays)
     parts = ()
     for stage in range(9):
@@ -394,15 +416,13 @@
         copy.wait()
 
 
-def neighbours(axis):
+def exchange(pair, other, axis):
     count = lax.axis_size(axis)
-    forward = [(i, i + 1) for i in range(count - 1)]
-    return forward, [(target, source) for source, target in forward]
-
-
-def swap(up, down, axis):
-    forward, backward = neighbours(axis)
-    return lax.ppermute(up, axis, forward), lax.ppermute(down, axis, backward)
+
+    def swap(buffer, first):
+        couples = [(i, i + 1) for i in range(first, count - 1, 2)]
+        return lax.ppermute(buffer, axis, couples + [(b, a) for a, b in couples])
+    return swap(pair, 0), swap(other, 1)
 
 
 def local(right_side, phase, table):
@@ -424,24 +444,24 @@
         return call(functools.partial(pack_kernel, width), name,
                     [shape(2, NB * width, HALF)] * 2 + [block], [VM], (source,))
 
-    up_l, down_l, label = pack(phase, HL, "packlabel")
-    up_f, down_f, field = pack(right_side, HB, "packfield")
-    low_l, high_l = swap(up_l, down_l, "gy")
-    low_f, high_f = swap(up_f, down_f, "gy")
+    *sent, label = pack(phase, HL, "packlabel")
+    got_label = exchange(*sent, "gy")
+    *sent, field = pack(right_side, HB, "packfield")
+    got_field = exchange(*sent, "gy")
     (label,) = call(join_label_kernel, "joinlabel", [block], [VM] * 3,
-                    (low_l, high_l, label), alias={2: 0})
+                    (*got_label, label), alias={2: 0})
     arrays = call(own_kernel, "own", state, [SM, VM], (table, label), cost=5)
-    field, up, down = call(
+    field, *sent = call(
         join_field_kernel, "joinfield", [block] + [shape(2, SENT, HALF)] * 2,
-        [VM] * 5, (low_f, high_f, label, arrays[9], field), alias={4: 0})
-    low, high = swap(up, down, "gx")
+        [VM] * 5, (*got_field, label, arrays[9], field), alias={4: 0})
+    got = exchange(*sent, "gx")
     *mats, t, z, u = arrays
     *refs, sums = call(
         inner_kernel, "inner", state[7:] + [brick] * 6 + [line], [VM] * 12,
         (right_side, field, *mats, t, z, u), cost=10, alias={9 + k: k for k in range(3)})
     *refs, sums = call(
         outer_kernel, "outer", state + [brick] * 6 + [line], [SM] + [VM] * 22,
-        (table, right_side, label, field, low, high, sums, *mats, *refs),
+        (table, right_side, label, field, *got, sums, *mats, *refs),
         cost=20, alias={7 + k: k for k in range(16)})
     r1, r2, r3, u0, u1, u2 = refs[10:]
     gathered = lax.all_to_all(

time: 79.4 us -> 71.8 us (0.904)
  starting transfers between devices: 17.6 us -> 12 us
  waiting for transfers between devices: 4.36 us -> 2.12 us
    ppermute x6, starting transfers between devices: 17.6 us -> 12 us  [swap(): return lax.ppermute(buffer, axis, couples + [(b, a) for a, b in couples])]
    ppermute x6, waiting for transfers between devices: 4.36 us -> 2.12 us  [swap(): return lax.ppermute(buffer, axis, couples + [(b, a) for a, b in couples])]
  transfers between devices with their start and end apart: 6 -> 6, of which waited for: 3 -> 2; matrix products, arithmetic and copies ran while one was open for 0% -> 0% of each run, Pallas kernels for 21% -> 22%
where the time goes in v4:
time: 71.8 us; the launch traced here: 71.6 us
  Pallas kernels  30.4 us (42%)
  blocking collectives  23.6 us (33%)
  starting transfers between devices  12 us (17%)
  local copies, waits for them, and re-layouts  2.49 us (3%)
  waiting for transfers between devices  2.12 us (3%)
  between operations  0.94 us (1%)
    pallas_call x7, Pallas kernels, call(): pl.pallas_call(kernel, name=name, in_specs=ins, out_specs=[VM] * len(outs...  27.9 us
    all_to_all x1, blocking collectives, local(): lax.all_to_all(jnp.broadcast_to(sums[0:1], (128, 128)), ('gx', 'gy'), 0,...  23.6 us
    ppermute x6, starting transfers between devices, swap(): return lax.ppermute(buffer, axis, couples + [(b, a) for a, b in couples])  12 us
    pallas_call x1, Pallas kernels, local(): pl.pallas_call(final_kernel, name='final', in_specs=[VM] * 8, out_specs=[...  2.53 us
    unnamed x8, local copies, waits for them, and re-layouts  2.45 us
    ppermute x6, waiting for transfers between devices, swap(): return lax.ppermute(buffer, axis, couples + [(b, a) for a, b in couples])  2.12 us
  transfers between devices with their start and end apart: 6, of which 2 were waited for; matrix products, arithmetic and copies ran while one was open for 0% of the time, Pallas kernels for 22%

profile of v4, /device:TPU:1, one launch (start us, length us, event | category | flops | bytes accessed | tf_op | source)
XLA Modules:
  0.0 71.6 jit_solution(2962750629701629035)
XLA Ops:
  0.6 0.0 copy-start.2
  0.6 1.2 %copy-done.2 = s32[32,32,256]{2,1,0:T(8,128)S(1)} copy-done((s32[32,32,256]{2,1,0:T(8,128)S(1)}, s32[32,32,256]{2,1,0:T(8,128)}, u32[]{:S(2)}) %copy-start.2) | copy-done | bytes 1048600
  1.9 0.0 copy-start.3
  1.9 0.2 packlabel.1
  2.1 2.1 %collective-permute-start = (f32[2,320,128]{2,1,0:T(8,128)S(1)}, f32[2,320,128]{2,1,0:T(8,128)S(1)}, u32[]{:S(2)}, u32[]{:S(2)}) collective-permute-start(f32[2,320,128]{2,1,0:T(8,128)S(1)} %get-tuple-element.40), channel_id=1, source_target_pairs={{0,1},{2,3},{4,5},{6,7},{8,9},{10,11},{12,13},{14,15},{1,0},{3,2},... | collective-permute-start | bytes 983048 | tf_op jit(solution)/shard_map/ppermute | solution.py:424
  4.2 0.7 collective-permute-start.1
  4.9 0.0 copy-start
  4.9 1.2 %copy-done = f32[32,32,256]{2,1,0:T(8,128)S(1)} copy-done((f32[32,32,256]{2,1,0:T(8,128)S(1)}, f32[32,32,256]{2,1,0:T(8,128)}, u32[]{:S(2)}) %copy-start) | copy-done | bytes 1048600
  6.1 0.2 packfield.1
  6.3 3.4 %collective-permute-start.2 = (f32[2,288,128]{2,1,0:T(8,128)S(1)}, f32[2,288,128]{2,1,0:T(8,128)S(1)}, u32[]{:S(2)}, u32[]{:S(2)}) collective-permute-start(f32[2,288,128]{2,1,0:T(8,128)S(1)} %get-tuple-element.43), channel_id=1, source_target_pairs={{0,1},{2,3},{4,5},{6,7},{8,9},{10,11},{12,13},{14,15},{1,0},{3,2},... | collective-permute-start | bytes 884744 | tf_op jit(solution)/shard_map/ppermute | solution.py:424
  9.7 0.7 collective-permute-start.3
  10.4 0.8 %collective-permute-done.pair = f32[2,320,128]{2,1,0:T(8,128)S(1)} collective-permute-done((f32[2,320,128]{2,1,0:T(8,128)S(1)}, f32[2,320,128]{2,1,0:T(8,128)S(1)}, u32[]{:S(2)}, u32[]{:S(2)}) %collective-permute-start) | collective-permute-done | bytes 327712 | tf_op jit(solution)/shard_map/ppermute | solution.py:424
  11.2 0.0 collective-permute-done.1.other
  11.2 0.1 joinlabel.1.label
  11.3 0.0 copy-done.3
  11.3 4.8 %own.1 = (f32[52,2,56,128]{3,2,1,0:T(8,128)S(1)}, f32[52,2,56,128]{3,2,1,0:T(8,128)S(1)}, f32[52,2,56,128]{3,2,1,0:T(8,128)S(1)}, f32[52,2,56,128]{3,2,1,0:T(8,1...) custom-call(f32[4]{0:T(128)S(1)} %copy-done.3, ...), custom_call_target="tpu_custom_call" | custom-call | bytes 12500000 | tf_op jit(solution)/shard_map/own/pallas_call | solution.py:430
  16.1 1.3 %collective-permute-done.2.pair = f32[2,288,128]{2,1,0:T(8,128)S(1)} collective-permute-done((f32[2,288,128]{2,1,0:T(8,128)S(1)}, f32[2,288,128]{2,1,0:T(8,128)S(1)}, u32[]{:S(2)}, u32[]{:S(2)}) %collective-permute-start.2) | collective-permute-done | bytes 294944 | tf_op jit(solution)/shard_map/ppermute | solution.py:424
  17.5 0.0 collective-permute-done.3.other
  17.5 0.2 joinfield.1
  17.7 1.8 %collective-permute-start.4 = (f32[2,776,128]{2,1,0:T(8,128)S(1)}, f32[2,776,128]{2,1,0:T(8,128)S(1)}, u32[]{:S(2)}, u32[]{:S(2)}) collective-permute-start(f32[2,776,128]{2,1,0:T(8,128)S(1)} %get-tuple-element.48), channel_id=1, source_target_pairs={{0,16},{32,48},{64,80},{96,112},{16,0},{48,32},{80,64},{112,96},{1... | collective-permute-start | bytes 2383880 | tf_op jit(solution)/shard_map/ppermute | solution.py:424
  19.4 3.4 %collective-permute-start.5 = (f32[2,776,128]{2,1,0:T(8,128)S(1)}, f32[2,776,128]{2,1,0:T(8,128)S(1)}, u32[]{:S(2)}, u32[]{:S(2)}) collective-permute-start(f32[2,776,128]{2,1,0:T(8,128)S(1)} %get-tuple-element.49), channel_id=1, source_target_pairs={{16,32},{48,64},{80,96},{32,16},{64,48},{96,80},{17,33},{49,65},{8... | collective-permute-start | bytes 2383880 | tf_op jit(solution)/shard_map/ppermute | solution.py:424
  22.8 10.9 %inner.1 = (f32[52,2,72,128]{3,2,1,0:T(8,128)S(1)}, f32[52,2,72,128]{3,2,1,0:T(8,128)S(1)}, f32[52,2,72,128]{3,2,1,0:T(8,128)S(1)}, f32[32,32,256]{2,1,0:T(8,128...) custom-call(f32[32,32,256]{2,1,0:T(8,128)S(1)} %copy-done, ...), custom_call_target="tpu_custom_call", output_to_operand_aliasing={{0}: (9, {}), {1}: (10, {}), {2}: (11, {})} | custom-call | bytes 25000000 | tf_op jit(solution)/shard_map/inner/pallas_call | solution.py:430
  33.7 0.0 collective-permute-done.4.pair
  33.7 0.0 collective-permute-done.5.other
  33.8 0.0 copy-start.1
  33.8 11.4 %outer.1 = (f32[52,2,56,128]{3,2,1,0:T(8,128)S(1)}, f32[52,2,56,128]{3,2,1,0:T(8,128)S(1)}, f32[52,2,56,128]{3,2,1,0:T(8,128)S(1)}, f32[52,2,56,128]{3,2,1,0:T(8...) custom-call(f32[4]{0:T(128)S(1)} %copy-done.3, ...), custom_call_target="tpu_custom_call", output_to_operand_aliasing={{0}: (7, {}), {1}: (8, {}), {2}: (9, {}), {3}: (10, {}), {4... | custom-call | bytes 50000000 | tf_op jit(solution)/shard_map/outer/pallas_call | solution.py:430
  45.3 23.6 %all_to_all.8 = f32[128,1,128]{2,1,0:T(1,128)S(1)} all-to-all(f32[128,1,128]{2,1,0:T(1,128)S(1)} %broadcast_in_dim.2), channel_id=1, replica_groups=mesh['gx'=8,'gy'=16] {'gx','gy'}, dimensions={0} | all-to-all | bytes 131072 | tf_op jit(solution)/shard_map/all_to_all | solution.py:467
  68.9 0.0 copy-done.1
  68.9 2.5 %final.1 = (f32[32,32,256]{2,1,0:T(8,128)}, f32[32,32,256]{2,1,0:T(8,128)}, f32[32,32,256]{2,1,0:T(8,128)}, f32[32,32,256]{2,1,0:T(8,128)}) custom-call(f32[128,128]{1,0:T(8,128)S(1)} %bitcast.3, f32[32,32,256]{2,1,0:T(8,128)S(1)} %copy-done.1, f32[32,32,256]{2,1,0:T(8,128)S(1)} %get-tuple-element.70.r1, f32[32,32,256]{2,1,0:T(8,128)S(1)} %get-tuple-element.71.r2, ...), custom_call_target="tpu_custom_call" | custom-call | tf_op jit(solution)/shard_map/final/pallas_call | solution.py:470
  (2 shorter events, 0.0 us)
Async XLA Ops:
  0.6 1.2 %copy-start.2 = (s32[32,32,256]{2,1,0:T(8,128)S(1)}, s32[32,32,256]{2,1,0:T(8,128)}, u32[]{:S(2)}) copy-start(s32[32,32,256]{2,1,0:T(8,128)} %source.2) | copy-start | bytes 3145732
  1.9 9.4 %copy-start.3 = (f32[4]{0:T(128)S(1)}, f32[4]{0:T(128)}, u32[]{:S(2)}) copy-start(f32[4]{0:T(128)} %table.3) | copy-start | bytes 52
  2.1 9.1 %collective-permute-start = (f32[2,320,128]{2,1,0:T(8,128)S(1)}, f32[2,320,128]{2,1,0:T(8,128)S(1)}, u32[]{:S(2)}, u32[]{:S(2)}) collective-permute-start(f32[2,320,128]{2,1,0:T(8,128)S(1)} %get-tuple-element.40), channel_id=1, source_target_pairs={{0,1},{2,3},{4,5},{6,7},{8,9},{10,11},{12,13},{14,15},{1,0},{3,2},... | collective-permute-start | bytes 983048 | tf_op jit(solution)/shard_map/ppermute | solution.py:424
  4.2 7.0 %collective-permute-start.1 = (f32[2,320,128]{2,1,0:T(8,128)S(1)}, f32[2,320,128]{2,1,0:T(8,128)S(1)}, u32[]{:S(2)}, u32[]{:S(2)}) collective-permute-start(f32[2,320,128]{2,1,0:T(8,128)S(1)} %get-tuple-element.41), channel_id=1, source_target_pairs={{1,2},{3,4},{5,6},{7,8},{9,10},{11,12},{13,14},{2,1},{4,3},{6,5},{... | collective-permute-start | bytes 983048 | tf_op jit(solution)/shard_map/ppermute | solution.py:424
  4.9 1.2 %copy-start = (f32[32,32,256]{2,1,0:T(8,128)S(1)}, f32[32,32,256]{2,1,0:T(8,128)}, u32[]{:S(2)}) copy-start(f32[32,32,256]{2,1,0:T(8,128)} %r0.1) | copy-start | bytes 3145732
  6.3 11.2 %collective-permute-start.2 = (f32[2,288,128]{2,1,0:T(8,128)S(1)}, f32[2,288,128]{2,1,0:T(8,128)S(1)}, u32[]{:S(2)}, u32[]{:S(2)}) collective-permute-start(f32[2,288,128]{2,1,0:T(8,128)S(1)} %get-tuple-element.43), channel_id=1, source_target_pairs={{0,1},{2,3},{4,5},{6,7},{8,9},{10,11},{12,13},{14,15},{1,0},{3,2},... | collective-permute-start | bytes 884744 | tf_op jit(solution)/shard_map/ppermute | solution.py:424
  9.7 7.8 %collective-permute-start.3 = (f32[2,288,128]{2,1,0:T(8,128)S(1)}, f32[2,288,128]{2,1,0:T(8,128)S(1)}, u32[]{:S(2)}, u32[]{:S(2)}) collective-permute-start(f32[2,288,128]{2,1,0:T(8,128)S(1)} %get-tuple-element.44), channel_id=1, source_target_pairs={{1,2},{3,4},{5,6},{7,8},{9,10},{11,12},{13,14},{2,1},{4,3},{6,5},{... | collective-permute-start | bytes 884744 | tf_op jit(solution)/shard_map/ppermute | solution.py:424
  17.7 16.0 %collective-permute-start.4 = (f32[2,776,128]{2,1,0:T(8,128)S(1)}, f32[2,776,128]{2,1,0:T(8,128)S(1)}, u32[]{:S(2)}, u32[]{:S(2)}) collective-permute-start(f32[2,776,128]{2,1,0:T(8,128)S(1)} %get-tuple-element.48), channel_id=1, source_target_pairs={{0,16},{32,48},{64,80},{96,112},{16,0},{48,32},{80,64},{112,96},{1... | collective-permute-start | bytes 2383880 | tf_op jit(solution)/shard_map/ppermute | solution.py:424
  19.4 14.3 %collective-permute-start.5 = (f32[2,776,128]{2,1,0:T(8,128)S(1)}, f32[2,776,128]{2,1,0:T(8,128)S(1)}, u32[]{:S(2)}, u32[]{:S(2)}) collective-permute-start(f32[2,776,128]{2,1,0:T(8,128)S(1)} %get-tuple-element.49), channel_id=1, source_target_pairs={{16,32},{48,64},{80,96},{32,16},{64,48},{96,80},{17,33},{49,65},{8... | collective-permute-start | bytes 2383880 | tf_op jit(solution)/shard_map/ppermute | solution.py:424
  33.8 35.1 %copy-start.1 = (f32[32,32,256]{2,1,0:T(8,128)S(1)}, f32[32,32,256]{2,1,0:T(8,128)}, u32[]{:S(2)}) copy-start(f32[32,32,256]{2,1,0:T(8,128)} %r0.1) | copy-start | bytes 3145732
